TPU v7x, 256 devices: a whole 4x4x8 slice. The times are simulated.
256 devices in a mesh: group: 128 (over z, y, x), seq: 2 (over core).
Axes of the slice: x: 4, y: 4, z: 8, core: 2. Of those that a mesh axis runs over, the one named last changes fastest.
Arguments:
- tokens: bfloat16 [65536, 1024], P(('group', 'seq')), may hold values from -12 to 12
- w_query: bfloat16 [1024, 1024], P(None, 'seq'), may hold values from -12.5 to 12.5
- w_key: bfloat16 [1024, 1024], P(None, 'seq'), may hold values from -0.1875 to 0.1875
- w_value: bfloat16 [1024, 1024], P(None, 'seq'), may hold values from -0.1875 to 0.1875
- w_out: bfloat16 [1024, 1024], P(None, 'seq'), may hold values from -0.1875 to 0.1875
- slot_query: bfloat16 [64, 1024], P(None, 'seq'), may hold values from -1300 to 1300
- span_decay: float32 [128, 8], P('group', 'seq'), may hold values from 0 to 6.7, as said below
- ffn_up: bfloat16 [1024, 4096], P('group', 'seq'), may hold values from -0.1875 to 0.1875
- ffn_down: bfloat16 [4096, 1024], P('seq', 'group'), may hold values from -0.09375 to 0.09375
- norm_gain: float32 [1024], replicated, may hold values from 0.5 to 1.5
Outputs:
- outputs: bfloat16 [65536, 1024], P('group', 'seq')
Inputs may be any that keep to these rules, and one draw needn't show every extreme that they name: `span_decay`: nonnegative per-span log decays.
All inputs are finite; a program needn't handle non-finite values.
Results may differ from a plain program's by a relative error of at most 0.02.
The roundings to bfloat16 on the way count: a program that leaves them out, or rounds other values in their place, can miss the bound.
Values may be sent and summed in bfloat16 or wider, within the bound.
A program may use at most 128 MiB of HBM per device.

v0:
```python
import jax
import jax.numpy as jnp
from jax import lax
from jax.sharding import PartitionSpec as P

HS = 128
MEM = 64
WIN = 512


floor_logit = -1e30
null_logit = 8.0


def prefix_2(value, axis, join, neutral):
    count, mine = (lax.axis_size(axis), lax.axis_index(axis))
    pieces = jax.tree.map(lambda part: lax.all_gather(part, axis), value)
    running = jax.tree.map(
        lambda part, zero: jnp.full_like(part, 0) + jnp.asarray(zero, part.dtype), value, neutral
    )

    def step(position, running):
        longer = join(running, jax.tree.map(lambda part: part[position], pieces))
        return jax.tree.map(lambda new, old: jnp.where(position < mine, new, old), longer, running)

    return lax.fori_loop(0, count - 1, step, running)


def passed_along(block, axis, distance):
    devices = range(lax.axis_size(axis))
    route = [(i - distance, i) for i in devices if i - distance in devices]
    return lax.ppermute(block, axis, route)


def merge_states(earlier, later_state):
    rate_a, peak_a, mass_a, value_a = earlier
    rate_b, peak_b, mass_b, value_b = later_state
    shifted = peak_a - rate_b[..., None]
    highest = jnp.maximum(shifted, peak_b)
    factor_a = jnp.exp(shifted - highest)
    factor_b = jnp.exp(peak_b - highest)
    return (
        rate_a + rate_b,
        highest,
        mass_a * factor_a + mass_b * factor_b,
        value_a * factor_a[..., None] + value_b * factor_b[..., None],
    )


def finish_memory(state):
    rate_sum, peak_val, mass_sum, weighted = state
    anchor = jnp.maximum(peak_val, null_logit)
    factor = jnp.exp(peak_val - anchor)
    denom = mass_sum * factor + jnp.exp(null_logit - anchor)
    return weighted * (factor / denom)[..., None]


def settle(memory, ffn_total, norm_gain):
    summed = memory.astype(jnp.float32) + ffn_total
    scaled = summed * lax.rsqrt(jnp.mean(summed * summed, axis=-1, keepdims=True) + 1e-06)
    return (scaled * norm_gain).astype(jnp.bfloat16)


def window_block(block_queries, block_keys, block_values, first_valid, mem_keys, mem_values):
    scale = HS ** (-0.5)
    scores = (
        jnp.einsum("qhd,khd->hqk", block_queries, block_keys, preferred_element_type=jnp.float32)
        * scale
    )
    row_pos = jnp.arange(WIN, dtype=jnp.int32)[:, None]
    col_pos = jnp.arange(2 * WIN, dtype=jnp.int32)[None, :]
    allowed = (col_pos > row_pos) & (col_pos <= row_pos + WIN) & (col_pos >= first_valid)
    scores = jnp.where(allowed[None], scores, floor_logit)
    probs = jnp.exp(scores - jnp.max(scores, axis=-1, keepdims=True))
    probs = probs / jnp.sum(probs, axis=-1, keepdims=True)
    local_out = jnp.einsum(
        "hqk,khd->qhd", probs.astype(jnp.bfloat16), block_values, preferred_element_type=jnp.float32
    )
    cross = (
        jnp.einsum("qhd,phd->hqp", block_queries, mem_keys, preferred_element_type=jnp.float32)
        * scale
    )
    cross_probs = jnp.exp(cross - jnp.max(cross, axis=-1, keepdims=True))
    cross_probs = cross_probs / jnp.sum(cross_probs, axis=-1, keepdims=True)
    cross_out = jnp.einsum(
        "hqp,phd->qhd",
        cross_probs.astype(jnp.bfloat16),
        mem_values,
        preferred_element_type=jnp.float32,
    )
    return (local_out + cross_out).astype(jnp.bfloat16)


def shards(
    tokens, w_query, w_key, w_value, w_out, slot_query, span_decay, ffn_up, ffn_down, norm_gain
):
    seq_count = lax.axis_size("seq")
    head_cols = w_query.shape[1]
    heads_dev = head_cols // HS
    span_len = tokens.shape[0] * seq_count
    span_idx = lax.axis_index("group")
    joined = jnp.concatenate([w_query, w_key, w_value], 1)
    projected = jnp.dot(
        lax.all_gather(tokens, "seq", axis=0, tiled=True),
        joined,
        preferred_element_type=jnp.float32,
    ).astype(jnp.bfloat16)
    queries = projected[:, :head_cols]
    keys_dev = projected[:, head_cols : 2 * head_cols]
    values_dev = projected[:, 2 * head_cols :]
    queries = queries.reshape(span_len, heads_dev, HS)
    keys_dev = keys_dev.reshape(span_len, heads_dev, HS)
    values_dev = values_dev.reshape(span_len, heads_dev, HS)
    slots = slot_query.reshape(MEM, heads_dev, HS)
    scores = jnp.einsum(
        "phd,thd->hpt", slots, keys_dev, preferred_element_type=jnp.float32
    ) * HS ** (-0.5)
    peak_val = jnp.max(scores, axis=-1)
    weights = jnp.exp(scores - peak_val[..., None])
    mass_sum = jnp.sum(weights, axis=-1)
    weighted = jnp.einsum(
        "hpt,thd->hpd", weights.astype(jnp.bfloat16), values_dev, preferred_element_type=jnp.float32
    )
    rate_now = span_decay[0]
    identity = (
        jnp.zeros((heads_dev,), jnp.float32),
        jnp.full((heads_dev, MEM), floor_logit, jnp.float32),
        jnp.zeros((heads_dev, MEM), jnp.float32),
        jnp.zeros((heads_dev, MEM, HS), jnp.float32),
    )
    prefix = prefix_2((rate_now, peak_val, mass_sum, weighted), "group", merge_states, identity)
    mem_local = (
        finish_memory(prefix).astype(jnp.bfloat16).transpose(1, 0, 2).reshape(MEM, head_cols)
    )
    mem_full = lax.all_gather(mem_local, "seq", axis=1, tiled=True)
    up_total = jnp.dot(
        mem_full,
        lax.all_gather(ffn_up, "group", axis=0, tiled=True),
        preferred_element_type=jnp.float32,
    )
    hidden = jax.nn.gelu(up_total).astype(jnp.bfloat16)
    partial_value = jnp.dot(
        hidden,
        lax.all_gather(ffn_down, "group", axis=1, tiled=True),
        preferred_element_type=jnp.float32,
    )
    summed = lax.psum(partial_value, "seq")
    settled = settle(mem_full, summed, norm_gain)
    mem_keys = (
        jnp.dot(settled, w_key, preferred_element_type=jnp.float32)
        .astype(jnp.bfloat16)
        .reshape(MEM, heads_dev, HS)
    )
    mem_values = (
        jnp.dot(settled, w_value, preferred_element_type=jnp.float32)
        .astype(jnp.bfloat16)
        .reshape(MEM, heads_dev, HS)
    )
    tail = jnp.stack([keys_dev, values_dev], 0)
    prior = passed_along(tail, "group", 1)
    ext_keys = jnp.concatenate([prior[0], keys_dev], 0)
    ext_values = jnp.concatenate([prior[1], values_dev], 0)
    blocks = span_len // WIN

    def attend(block_index):
        first_row = block_index * WIN
        first_valid = WIN - span_idx * span_len - first_row
        return window_block(queries, ext_keys, ext_values, first_valid, mem_keys, mem_values)

    mixed = lax.map(attend, jnp.arange(blocks, dtype=jnp.int32)).reshape(span_len, head_cols)
    result = jnp.dot(
        lax.all_gather(mixed, "seq", axis=1, tiled=True), w_out, preferred_element_type=jnp.float32
    )
    return result.astype(jnp.bfloat16)


def solution(mesh):
    in_specs = (
        P(("group", "seq"), None),
        P(None, "seq"),
        P(None, "seq"),
        P(None, "seq"),
        P(None, "seq"),
        P(None, "seq"),
        P("group", "seq"),
        P("group", "seq"),
        P("seq", "group"),
        P(),
    )
    out_specs = P("group", "seq")
    return jax.shard_map(shards, mesh=mesh, in_specs=in_specs, out_specs=out_specs, check_vma=False)
```

profile of v0, /device:TPU:1, one launch (start us, length us, event | category | flops | bytes accessed | tf_op | source)
XLA Modules:
  0.0 1323.6 jit_solution(15887826875648182784)
XLA Ops:
  7.3 20.7 %all-gather.12.cloned.1.call-done = bf16[512,1024]{1,0:T(8,128)(2,1)} async-done(((bf16[256,1024]{1,0:T(8,128)(2,1)}), bf16[512,1024]{1,0:T(8,128)(2,1)}) %all-gather.12.cloned.1.call-update) | async-done | bytes 1048592 | tf_op jit(solution)/shard_map/all_gather | solution.py:104
  28.0 4.0 fusion.22
  36.3 2.3 pad_maximum_fusion
  38.6 3.8 collective-permute-start
  42.6 306.4 %all-gather.3 = f32[128,1,4]{2,1,0:T(1,128)S(1)} all-gather(f32[1,1,4]{2,1,0:T(1,128)S(1)} %bitcast.108), channel_id=1, replica_groups=mesh['group'=128,'seq'=2] {'group'}, dimensions={0}, use_global_device_ids=true | all-gather | bytes 2064 | tf_op jit(solution)/shard_map/all_gather | solution.py:17
  349.0 1.3 fusion.26
  352.4 284.2 %all-gather.5 = f32[128,4,64]{2,1,0:T(4,128)S(1)} all-gather(f32[1,4,64]{2,1,0:T(4,128)S(1)} %bitcast.107), channel_id=3, replica_groups=mesh['group'=128,'seq'=2] {'group'}, dimensions={0}, use_global_device_ids=true | all-gather | bytes 132096 | tf_op jit(solution)/shard_map/all_gather | solution.py:17
  636.7 285.5 %all-gather.4 = f32[128,4,64]{2,1,0:T(4,128)S(1)} all-gather(f32[1,4,64]{2,1,0:T(4,128)S(1)} %bitcast.105), channel_id=2, replica_groups=mesh['group'=128,'seq'=2] {'group'}, dimensions={0}, use_global_device_ids=true | all-gather | bytes 132096 | tf_op jit(solution)/shard_map/all_gather | solution.py:17
  922.2 2.1 slice_bitcast_fusion.1
  924.3 4.5 fusion.37
  928.8 156.2 %while.22 = (s32[]{:T(128)}, f32[4,64]{1,0:T(4,128)S(1)}, f32[4,64]{1,0:T(4,128)S(1)}, f32[4,64,128]{2,1,0:T(8,128)S(1)}, s32[]{:T(128)}, /*index=5*/f32[128,4]{...) while((s32[]{:T(128)}, f32[4,64]{1,0:T(4,128)S(1)}, ...), condition=%wide.region_5.6_spmd.clone, body=%wide.region_4.5_spmd.clone.sunk | while | flops 166660 | bytes 403647 | solution.py:26
  928.9 1.1 fusion.113
  932.6 1.1 fusion.113
  936.3 1.1 fusion.113
  940.0 1.1 fusion.113
  944.9 1.1 fusion.113
  948.6 1.1 fusion.113
  952.3 1.1 fusion.113
  956.0 1.1 fusion.113
  959.7 1.1 fusion.113
  963.4 1.1 fusion.113
  968.3 1.1 fusion.113
  972.0 1.1 fusion.113
  1085.2 167.4 %all_gather.44 = bf16[64,1024]{1,0:T(8,128)(2,1)S(1)} all-gather(bf16[64,512]{1,0:T(8,128)(2,1)S(1)} %copy_bitcast_fusion), channel_id=1, replica_groups=mesh['group'=128,'seq'=2] {'seq'}, dimensions={1}, use_global_device_ids=true | all-gather | bytes 196608 | tf_op jit(solution)/shard_map/all_gather | solution.py:135
  1252.6 6.4 fusion.54
  1259.3 13.0 fusion.87
  1272.3 13.9 %all-reduce.2.cloned.1.call-done = f32[64,1024]{1,0:T(8,128)} async-done(((f32[64,1024]{1,0:T(8,128)}), f32[64,1024]{1,0:T(8,128)}) %all-reduce.2.cloned.1.call-update) | async-done | bytes 262160 | tf_op jit(solution)/shard_map/psum | solution.py:147
  1288.7 1.6 fusion.32
  1290.6 1.4 fusion.53
  1292.0 6.1 fusion.28
  1298.1 15.8 %all-gather.18.cloned.1.call-done = bf16[512,1024]{0,1:T(8,128)(2,1)} async-done(((bf16[512,512]{0,1:T(8,128)(2,1)}), bf16[512,1024]{0,1:T(8,128)(2,1)}) %all-gather.18.cloned.1.call-update) | async-done | bytes 1048592 | tf_op jit(solution)/shard_map/all_gather | solution.py:172
  1314.0 2.8 convolution_convert_fusion
  (424 shorter events, 149.2 us)
Async XLA Ops:
  6.5 1307.4 %copy-start = (bf16[1024,512]{1,0:T(8,128)(2,1)S(1)}, bf16[1024,512]{1,0:T(8,128)(2,1)}, u32[]{:S(2)}) copy-start(bf16[1024,512]{1,0:T(8,128)(2,1)} %param.16) | copy-start | bytes 3145732
  6.5 21.5 %all-gather.12.cloned.1.call-start = ((), (), s32[]{:S(2)}) async-start(), calls=%async_computation | async-start | bytes 1572864 | tf_op jit(solution)/shard_map/all_gather | solution.py:104
  7.3 25.0 %copy-start.6 = (bf16[64,512]{1,0:T(8,128)(2,1)S(1)}, bf16[64,512]{1,0:T(8,128)(2,1)}, u32[]{:S(2)}) copy-start(bf16[64,512]{1,0:T(8,128)(2,1)} %param.17) | copy-start | bytes 196612
  7.3 921.6 %all-gather.20.cloned.1.call-start = ((), (), s32[]{:S(2)}) async-start(), calls=%async_computation.5 | async-start | bytes 16908288 | tf_op jit(solution)/shard_map/all_gather | solution.py:17
  32.1 10.5 copy-start.8
  33.5 1219.0 %all-gather.14.cloned.1.call-start = ((), (), s32[]{:S(2)}) async-start(), calls=%async_computation.1 | async-start | bytes 4227072 | tf_op jit(solution)/shard_map/all_gather | solution.py:138
  34.3 1218.3 %all-gather.16.cloned.1.call-start = ((), (), s32[]{:S(2)}) async-start(), calls=%async_computation.2 | async-start | bytes 4227072 | tf_op jit(solution)/shard_map/all_gather | solution.py:144
  38.6 883.6 %collective-permute-start = (bf16[2,512,4,128]{3,1,2,0:T(8,128)(2,1)}, bf16[2,512,4,128]{3,1,2,0:T(8,128)(2,1)}, u32[]{:S(2)}, u32[]{:S(2)}) collective-permute-start(bf16[2,512,4,128]{3,1,2,0:T(8,128)(2,1)} %pad_maximum_fusion), channel_id=1, source_target_pairs={{0,2},{2,4},{4,6},{6,8},{8,10},{10,12},{12,14},{14,16},{16,18},{18... | collective-permute-start | bytes 3145736 | tf_op jit(solution)/shard_map/ppermute | solution.py:32
  42.5 1243.7 %all-reduce.2.cloned.1.call-start = ((), (), s32[]{:S(2)}) async-start(), calls=%async_computation.3 | async-start | bytes 524288 | tf_op jit(solution)/shard_map/psum | solution.py:147
  351.2 573.1 %copy-start.1 = (bf16[512,4,128]{2,0,1:T(8,128)(2,1)S(1)}, bf16[512,4,128]{2,0,1:T(8,128)(2,1)}, u32[]{:S(2)}) copy-start(bf16[512,4,128]{2,0,1:T(8,128)(2,1)} %copy.27) | copy-start | bytes 1572868
  1252.6 6.7 copy-start.4
  1259.0 28.2 %copy-start.7 = (f32[1024]{0:T(1024)S(1)}, f32[1024]{0:T(1024)}, u32[]{:S(2)}) copy-start(f32[1024]{0:T(1024)} %param.21) | copy-start | bytes 12292
  1259.0 29.3 %copy-start.2 = (bf16[1024,512]{1,0:T(8,128)(2,1)S(1)}, bf16[1024,512]{1,0:T(8,128)(2,1)}, u32[]{:S(2)}) copy-start(bf16[1024,512]{1,0:T(8,128)(2,1)} %param.14) | copy-start | bytes 3145732
  1259.1 54.9 %all-gather.18.cloned.1.call-start = ((), (), s32[]{:S(2)}) async-start(), calls=%async_computation.4 | async-start | bytes 1572864 | tf_op jit(solution)/shard_map/all_gather | solution.py:172
  1272.3 19.7 %copy-start.3 = (bf16[512,4,128]{2,0,1:T(8,128)(2,1)S(1)}, bf16[512,4,128]{2,0,1:T(8,128)(2,1)}, u32[]{:S(2)}) copy-start(bf16[512,4,128]{2,0,1:T(8,128)(2,1)} %copy.26) | copy-start | bytes 1572868
  1288.7 3.4 copy-start.5
Sparse Core Ops, SparseCore 0:
  9.1 18.8 all-gather.11
  33.7 151.9 all-gather.19
  189.3 111.0 all-gather.13
  303.8 113.7 all-gather.15
  1259.2 26.9 all-reduce.1
  1298.2 15.6 all-gather.17
where the time goes:
time: 1330 us; the launch traced here: 1320 us
  blocking collectives  1040 us (78%)
  other arithmetic  170 us (13%)
  waiting for transfers between devices  51.9 us (4%)
  matrix products  28.6 us (2%)
  between operations  13.7 us (1%)
    all_gather x3, blocking collectives, prefix_2(): pieces = jax.tree.map(lambda part: lax.all_gather(part, axis), value)  876 us
    all_gather x1, blocking collectives, shards(): mem_full = lax.all_gather(mem_local, 'seq', axis=1, tiled=True)  167 us
    select_n x254, other arithmetic, step(): jnp.where(position < mine, new, old)  151 us
  transfers between devices with their start and end apart: 7, of which 3 were waited for; matrix products, arithmetic and copies ran while one was open for 14% of the time, Pallas kernels for 0%

commit v1 on v0

v1 whole, which is shorter than its diff:
```python
import jax
import jax.numpy as jnp
from jax import lax
from jax.experimental import pallas as pl
from jax.experimental.pallas import tpu as pltpu
from jax.sharding import PartitionSpec as P

HS = 128
MEM = 64
NX, NY, NZ = 4, 4, 8
NG = NX * NY * NZ
HALF = 256
HC = 512
HEADS = 4
D = 1024
PART = MEM // NX
ROWS = HEADS * PART
FS = 512
MESH = pl.DeviceIdType.MESH
F32 = jnp.float32
BF = jnp.bfloat16
FLOOR = -1e30
NULL = 8.0
SCALE = HS ** (-0.5)
LOG2E = 1.4426950408889634


def nn(a, b):
    return lax.dot_general(a, b, (((1,), (0,)), ((), ())), preferred_element_type=F32)


def nt(a, b):
    return lax.dot_general(a, b, (((1,), (1,)), ((), ())), preferred_element_type=F32)


def merge(a, b):
    rate_a, peak_a, mass_a, val_a = a
    rate_b, peak_b, mass_b, val_b = b
    shifted = peak_a - rate_b
    high = jnp.maximum(shifted, peak_b)
    fa = jnp.exp(shifted - high)
    fb = jnp.exp(peak_b - high)
    return (rate_a + rate_b, high, mass_a * fa + mass_b * fb, val_a * fa + val_b * fb)


def pick(cond, a, b):
    return tuple(jnp.where(cond, p, q) for p, q in zip(a, b))


def identity():
    z = jnp.zeros((ROWS, 1), F32)
    return (z, z + FLOOR, z, jnp.zeros((ROWS, HS), F32))


def stat_columns(peak, mass, rate, rows):
    lane = lax.broadcasted_iota(jnp.int32, (rows, 128), 1)
    return jnp.where(lane == 0, peak, jnp.where(lane == 1, mass, jnp.where(lane == 2, rate, 0.0)))


def encode(state):
    rate, peak, mass, _ = state
    cols = stat_columns(peak, mass, rate, ROWS)
    full = jnp.concatenate([cols, jnp.zeros((128 - ROWS, 128), F32)], 0)
    return jnp.transpose(full)[0:8]


def decode(tiles, count):
    flat = tiles.reshape(count * 8, 128)
    full = jnp.concatenate([flat, jnp.zeros((128 - count * 8, 128), F32)], 0)
    return jnp.transpose(full)


def column_state(cols, k, val):
    return (cols[:, 8 * k + 2 : 8 * k + 3], cols[:, 8 * k : 8 * k + 1], cols[:, 8 * k + 1 : 8 * k + 2], val)


def body(
    tok_h, wq_h, wk_h, wv_h, wo_h, slot_ref, decay_ref, up_h, dn_h, gain_ref, out_ref,
    tok, ptok, wq, wk, wv, wo, qs, ks, vs, kp, vp, up, dn,
    ps, pst, sc, xr, xst, yr, yst, zr, zst, fm, pb, rs, own, st, lo, mk, mv, mx,
    load_sem, loc_sem, tok_s, tok_r, wx_s, wx_r, wz_s, wz_r, wy_s, wy_r,
    x_s, x_r, y_s, y_r, z_s, z_r, fm_s, fm_r, rs_s, rs_r, st_s, st_r, mx_s, mx_r,
):
    g = lax.axis_index("group")
    c = lax.axis_index("seq")
    x = lax.rem(g, NX)
    y = lax.rem(g // NX, NY)
    z = g // (NX * NY)
    oc = 1 - c

    def gid(zz, yy, xx):
        return zz * (NX * NY) + yy * NX + xx

    def xp(d):
        return lax.rem(x + d, NX)

    def yp(d):
        return lax.rem(y + d, NY)

    def zp(d):
        return lax.rem(z + d, NZ)

    nxt = lax.rem(g + 1, NG)
    prv = lax.rem(g + NG - 1, NG)
    sends = []

    def send(src, dst, ss, rsem, gg, cc):
        cp = pltpu.make_async_remote_copy(
            src_ref=src, dst_ref=dst, send_sem=ss, recv_sem=rsem,
            device_id={"group": gg, "seq": cc}, device_id_type=MESH,
        )
        cp.start()
        sends.append(cp)
        return cp

    def arrived(ref, sem, ss):
        pltpu.make_async_remote_copy(
            src_ref=ref, dst_ref=ref, send_sem=ss, recv_sem=sem,
            device_id={"group": g, "seq": oc}, device_id_type=MESH,
        ).wait_recv()

    loads = []
    for k, (src, dst) in enumerate(
        ((tok_h, tok.at[c]), (wk_h, wk), (wv_h, wv), (wq_h, wq), (wo_h, wo))
    ):
        cp = pltpu.make_async_copy(src, dst, load_sem.at[k])
        cp.start()
        loads.append(cp)
    lanes_x = pl.ds(pl.multiple_of(x * FS, FS), FS)
    wl = []
    for k, (src, dst) in enumerate(((up_h, up), (dn_h, dn))):
        cp = pltpu.make_async_copy(src.at[:, lanes_x], dst.at[z, y, x], loc_sem.at[k])
        cp.start()
        wl.append(cp)

    barrier = pltpu.get_barrier_semaphore()

    def greet(gg, cc):
        pl.semaphore_signal(barrier, inc=1, device_id={"group": gg, "seq": cc}, device_id_type=MESH)

    greet(g, oc)
    for d in range(1, NX):
        greet(gid(z, y, xp(d)), c)
        greet(gid(z, y, xp(d)), oc)
    for d in range(1, NY):
        greet(gid(z, yp(d), x), c)
    for d in range(1, NZ):
        greet(gid(zp(d), y, x), c)
    greet(nxt, c)
    greet(prv, c)

    def project(half):
        rows = tok[half]
        ks[half] = nn(rows, wk[...]).astype(BF)
        vs[half] = nn(rows, wv[...]).astype(BF)
        qs[half] = nn(rows, wq[...]).astype(BF)

    pl.semaphore_wait(barrier, 2 * (NX - 1) + (NY - 1) + (NZ - 1) + 3)

    send(tok_h, tok.at[c], tok_s.at[0], tok_r.at[0], g, oc)
    for k, (src, dst) in enumerate(((up_h, up), (dn_h, dn))):
        for d in range(1, NX):
            to = xp(d)
            send(
                src.at[:, pl.ds(pl.multiple_of(to * FS, FS), FS)], dst.at[z, y, x],
                wx_s.at[k, d - 1], wx_r.at[k, d - 1], gid(z, y, to), c,
            )
    send(tok_h, ptok.at[c], tok_s.at[1], tok_r.at[1], nxt, c)

    for cp in loads[:4]:
        cp.wait()
    project(c)

    def weights_z(k, buf):
        wl[k].wait()
        for d in range(1, NX):
            arrived(buf.at[z, y, xp(NX - d)], wx_r.at[k, d - 1], wx_s.at[k, d - 1])
        for d in range(1, NZ):
            send(
                buf.at[z, y], buf.at[z, y], wz_s.at[k, d - 1], wz_r.at[k, d - 1],
                gid(zp(d), y, x), c,
            )

    def weights_y(k, buf):
        for d in range(1, NZ):
            arrived(buf.at[zp(NZ - d), y], wz_r.at[k, d - 1], wz_s.at[k, d - 1])
        for d in range(1, NY):
            send(
                buf.at[:, y], buf.at[:, y], wy_s.at[k, d - 1], wy_r.at[k, d - 1],
                gid(z, yp(d), x), c,
            )

    def weights_done(k, buf):
        for d in range(1, NY):
            arrived(buf.at[:, yp(NY - d)], wy_r.at[k, d - 1], wy_s.at[k, d - 1])

    weights_z(0, up)
    weights_z(1, dn)

    arrived(tok.at[oc], tok_r.at[0], tok_s.at[0])
    project(oc)

    for h in range(HEADS):
        cols = slice(h * HS, (h + 1) * HS)
        keys = ks[:, :, cols].reshape(2 * HALF, HS)
        vals = vs[:, :, cols].reshape(2 * HALF, HS)
        scores = nt(slot_ref[:, cols], keys) * SCALE
        peak = jnp.max(scores, axis=1, keepdims=True)
        w = jnp.exp(scores - peak)
        mass = jnp.sum(w, axis=1, keepdims=True)
        pooled = nn(w.astype(BF), vals)
        stat = stat_columns(peak, mass, decay_ref[0:1, h : h + 1], MEM)
        for p in range(NX):
            rows = slice(p * PART, (p + 1) * PART)
            ps[p, h * PART : (h + 1) * PART, :] = pooled[rows]
            first = (p % 2) * ROWS + h * PART
            sc[p // 2, first : first + PART, :] = stat[rows]
    for q in range(2):
        pst[q] = jnp.transpose(sc[q])[0:8]

    for d in range(1, NX):
        to = xp(d)
        send(ps.at[to], xr.at[x], x_s.at[0, d - 1], x_r.at[0, d - 1], gid(z, y, to), c)
        send(pst.at[to // 2], xst.at[x], x_s.at[1, d - 1], x_r.at[1, d - 1], gid(z, y, to), c)
    xr[x] = ps[x]
    xst[x] = pst[x // 2]
    for d in range(1, NX):
        frm = xp(NX - d)
        arrived(xr.at[frm], x_r.at[0, d - 1], x_s.at[0, d - 1])
        arrived(xst.at[frm], x_r.at[1, d - 1], x_s.at[1, d - 1])
    both = decode(xst[...], NX)
    cols = jnp.where(lax.rem(x, 2) == 0, both[0:ROWS], both[ROWS : 2 * ROWS])
    in_row = [identity()]
    total = column_state(cols, 0, xr[0])
    for j in range(1, NX):
        in_row.append(total)
        total = merge(total, column_state(cols, j, xr[j]))

    yr[y] = total[3]
    yst[y] = encode(total)
    for d in range(1, NY):
        to = gid(z, yp(d), x)
        send(yr.at[y], yr.at[y], y_s.at[0, d - 1], y_r.at[0, d - 1], to, c)
        send(yst.at[y], yst.at[y], y_s.at[1, d - 1], y_r.at[1, d - 1], to, c)
    for d in range(1, NY):
        frm = yp(NY - d)
        arrived(yr.at[frm], y_r.at[0, d - 1], y_s.at[0, d - 1])
        arrived(yst.at[frm], y_r.at[1, d - 1], y_s.at[1, d - 1])
    cols = decode(yst[...], NY)[0:ROWS]
    in_plane = identity()
    total = None
    for j in range(NY):
        item = column_state(cols, j, yr[j])
        in_plane = pick(j < y, merge(in_plane, item), in_plane)
        total = item if total is None else merge(total, item)

    zr[z] = total[3]
    zst[z] = encode(total)
    for d in range(1, NZ):
        to = gid(zp(d), y, x)
        send(zr.at[z], zr.at[z], z_s.at[0, d - 1], z_r.at[0, d - 1], to, c)
        send(zst.at[z], zst.at[z], z_s.at[1, d - 1], z_r.at[1, d - 1], to, c)

    arrived(ptok.at[c], tok_r.at[1], tok_s.at[1])
    send(ptok.at[c], ptok.at[c], tok_s.at[2], tok_r.at[2], g, oc)

    def project_prev(half):
        rows = ptok[half]
        kp[half] = nn(rows, wk[...]).astype(BF)
        vp[half] = nn(rows, wv[...]).astype(BF)

    project_prev(c)
    weights_y(0, up)
    weights_y(1, dn)
    arrived(ptok.at[oc], tok_r.at[2], tok_s.at[2])
    project_prev(oc)

    row_i = lax.broadcasted_iota(jnp.int32, (HALF, HALF), 0)
    col_i = lax.broadcasted_iota(jnp.int32, (HALF, HALF), 1)
    tri = col_i <= row_i
    bias = jnp.where(g == 0, FLOOR, 0.0).astype(F32)

    def attend(h, i):
        cols = slice(h * HS, (h + 1) * HS)
        q = qs[i, :, cols]
        near = nt(q, ks[i, :, cols])
        far = nt(q, kp[i, :, cols]) + bias
        diag = jnp.where(tri, near, far)
        if i == 0:
            full = nt(q, kp[1, :, cols]) + bias
            full_v = vp[1, :, cols]
        else:
            full = nt(q, ks[0, :, cols])
            full_v = vs[0, :, cols]
        high = jnp.maximum(
            jnp.max(diag, axis=1, keepdims=True), jnp.max(full, axis=1, keepdims=True)
        )
        ed = jnp.exp2((diag - high) * (SCALE * LOG2E))
        ef = jnp.exp2((full - high) * (SCALE * LOG2E))
        mass = jnp.sum(ed, axis=1, keepdims=True) + jnp.sum(ef, axis=1, keepdims=True)
        acc = nn(jnp.where(tri, ed, 0.0).astype(BF), vs[i, :, cols])
        acc += nn(jnp.where(tri, 0.0, ed).astype(BF), vp[i, :, cols])
        acc += nn(ef.astype(BF), full_v)
        lo[i, :, cols] = acc / mass

    for h in range(HEADS):
        for i in range(2):
            attend(h, i)

    for d in range(1, NZ):
        frm = zp(NZ - d)
        arrived(zr.at[frm], z_r.at[0, d - 1], z_s.at[0, d - 1])
        arrived(zst.at[frm], z_r.at[1, d - 1], z_s.at[1, d - 1])
    cols = decode(zst[...], NZ)[0:ROWS]
    before = identity()
    for j in range(NZ):
        before = pick(j < z, merge(before, column_state(cols, j, zr[j])), before)
    before = merge(before, in_plane)
    for j in range(NX):
        _, peak, mass, val = merge(before, in_row[j])
        anchor = jnp.maximum(peak, NULL)
        factor = jnp.exp(peak - anchor)
        denom = mass * factor + jnp.exp(NULL - anchor)
        memory = (val * (factor / denom)).astype(BF)
        for h in range(HEADS):
            fm[c, x, j * PART : (j + 1) * PART, h * HS : (h + 1) * HS] = memory[
                h * PART : (h + 1) * PART
            ]
    k = 0
    row_peers = [(0, True)] + [(d, f) for d in range(1, NX) for f in (False, True)]
    for d, flip in row_peers:
        send(
            fm.at[c, x], fm.at[c, x], fm_s.at[k], fm_r.at[k],
            gid(z, y, xp(d)), oc if flip else c,
        )
        k += 1
    k = 0
    for d, flip in row_peers:
        arrived(fm.at[oc if flip else c, xp(NX - d) if d else x], fm_r.at[k], fm_s.at[k])
        k += 1

    weights_done(0, up)
    mem0 = fm[0].reshape(NX * MEM, HC)
    mem1 = fm[1].reshape(NX * MEM, HC)
    total = nn(mem0, up[0 : NZ // 2].reshape(D // 2, FS)) + nn(mem1, up[NZ // 2 :].reshape(D // 2, FS))
    hidden = jax.nn.gelu(total, approximate=True).astype(BF)
    weights_done(1, dn)
    part = nt(hidden, dn[...].reshape(D, FS))
    for j in range(NX):
        for cc in range(2):
            for q in range(2):
                first = (2 * cc + q) * MEM + j * PART
                piece = part[first : first + PART]
                own[j, cc, q * PART : (q + 1) * PART, :] = piece
                pb[j, cc, q * PART : (q + 1) * PART, :] = piece.astype(BF)
    k = 0
    for d, flip in row_peers:
        to = xp(d)
        cc = oc if flip else c
        send(pb.at[to, cc], rs.at[k], rs_s.at[k], rs_r.at[k], gid(z, y, to), cc)
        k += 1
    acc = own[x, c]
    mem = fm[:, pl.ds(2 * c, 2), pl.ds(pl.multiple_of(x * PART, PART), PART), :]
    mem = jnp.concatenate(
        [mem[0].reshape(2 * PART, HC), mem[1].reshape(2 * PART, HC)], 1
    ).astype(F32)
    for k in range(7):
        arrived(rs.at[k], rs_r.at[k], rs_s.at[k])
    for k in range(7):
        acc += rs[k].astype(F32)
    summed = mem + acc
    scaled = summed * lax.rsqrt(jnp.mean(summed * summed, axis=-1, keepdims=True) + 1e-06)
    st[c] = (scaled * gain_ref[...]).astype(BF)
    send(st.at[c], st.at[c], st_s, st_r, g, oc)
    arrived(st.at[oc], st_r, st_s)
    settled = st[...].reshape(MEM, D)
    mk[...] = nn(settled, wk[...]).astype(BF)
    mv[...] = nn(settled, wv[...]).astype(BF)

    for h in range(HEADS):
        cols = slice(h * HS, (h + 1) * HS)
        q = qs[:, :, cols].reshape(2 * HALF, HS)
        scores = nt(q, mk[:, cols])
        high = jnp.max(scores, axis=1, keepdims=True)
        e = jnp.exp2((scores - high) * (SCALE * LOG2E))
        probs = (e / jnp.sum(e, axis=1, keepdims=True)).astype(BF)
        cross = nn(probs, mv[:, cols])
        both = lo[:, :, cols].reshape(2 * HALF, HS) + cross
        mx[c, h] = both.astype(BF)
        send(mx.at[c, h], mx.at[c, h], mx_s.at[h], mx_r.at[h], g, oc)
    loads[4].wait()

    def out_part(cc, h):
        return nn(mx[cc, h], wo[pl.ds(pl.multiple_of(cc * HC + h * HS, HS), HS), :])

    acc = out_part(c, 0)
    for h in range(1, HEADS):
        acc += out_part(c, h)
    for h in range(HEADS):
        arrived(mx.at[oc, h], mx_r.at[h], mx_s.at[h])
        acc += out_part(oc, h)
    out_ref[...] = acc.astype(BF)

    for cp in sends:
        cp.wait_send()


def shards(tokens, w_query, w_key, w_value, w_out, slot_query, span_decay, ffn_up, ffn_down, norm_gain):
    V = pltpu.VMEM
    DMA = pltpu.SemaphoreType.DMA
    scratch = [
        V((2, HALF, D), BF), V((2, HALF, D), BF),
        V((D, HC), BF), V((D, HC), BF), V((D, HC), BF), V((D, HC), BF),
        V((2, HALF, HC), BF), V((2, HALF, HC), BF), V((2, HALF, HC), BF),
        V((2, HALF, HC), BF), V((2, HALF, HC), BF),
        V((NZ, NY, NX, 8, FS), BF), V((NZ, NY, NX, 8, FS), BF),
        V((NX, ROWS, HS), F32), V((2, 8, 128), F32), V((2, 128, 128), F32),
        V((NX, ROWS, HS), F32), V((NX, 8, 128), F32),
        V((NY, ROWS, HS), F32), V((NY, 8, 128), F32),
        V((NZ, ROWS, HS), F32), V((NZ, 8, 128), F32),
        V((2, NX, NX * PART, HC), BF),
        V((NX, 2, 2 * PART, D), BF), V((7, 2 * PART, D), BF), V((NX, 2, 2 * PART, D), F32),
        V((2, 2 * PART, D), BF),
        V((2, HALF, HC), F32),
        V((MEM, HC), BF), V((MEM, HC), BF),
        V((2, HEADS, 2 * HALF, HS), BF),
        DMA((5,)), DMA((2,)), DMA((3,)), DMA((3,)),
        DMA((2, NX - 1)), DMA((2, NX - 1)), DMA((2, NZ - 1)), DMA((2, NZ - 1)),
        DMA((2, NY - 1)), DMA((2, NY - 1)),
        DMA((2, NX - 1)), DMA((2, NX - 1)), DMA((2, NY - 1)), DMA((2, NY - 1)),
        DMA((2, NZ - 1)), DMA((2, NZ - 1)),
        DMA((7,)), DMA((7,)), DMA((7,)), DMA((7,)), DMA, DMA, DMA((HEADS,)), DMA((HEADS,)),
    ]
    hbm = pl.BlockSpec(memory_space=pl.ANY)
    vm = pl.BlockSpec(memory_space=pltpu.VMEM)
    return pl.pallas_call(
        body,
        out_shape=jax.ShapeDtypeStruct((2 * HALF, HC), BF),
        in_specs=[hbm, hbm, hbm, hbm, hbm, vm, vm, hbm, hbm, vm],
        out_specs=vm,
        scratch_shapes=scratch,
        compiler_params=pltpu.CompilerParams(
            collective_id=0, has_side_effects=True, vmem_limit_bytes=60 * 1024 * 1024
        ),
    )(
        tokens, w_query, w_key, w_value, w_out, slot_query, span_decay, ffn_up,
        ffn_down.T, norm_gain.reshape(1, D),
    )


def solution(mesh):
    in_specs = (
        P(("group", "seq"), None),
        P(None, "seq"),
        P(None, "seq"),
        P(None, "seq"),
        P(None, "seq"),
        P(None, "seq"),
        P("group", "seq"),
        P("group", "seq"),
        P("seq", "group"),
        P(),
    )
    out_specs = P("group", "seq")
    return jax.shard_map(shards, mesh=mesh, in_specs=in_specs, out_specs=out_specs, check_vma=False)
```

time: 1330 us -> 76.3 us (0.06)
  blocking collectives: 1040 us -> 0 us
  other arithmetic: 170 us -> 0 us
  Pallas kernels: 0 us -> 74.2 us
  waiting for transfers between devices: 51.9 us -> 0 us
  matrix products: 28.6 us -> 0 us
  between operations: 13.7 us -> 0.01 us
    all_gather x4 -> x0, blocking collectives: 1040 us -> none  [the longest x3 876 us: prefix_2(): pieces = jax.tree.map(lambda part: lax.all_gather(part, axis), value)]
    select_n x254 -> x0, other arithmetic: 151 us -> none  [step(): jnp.where(position < mine, new, old)]
    pallas_call x0 -> x1, Pallas kernels: none -> 74.2 us  [shards(): pl.pallas_call(body, out_shape=jax.ShapeDtypeStruct((2 * HALF, HC), BF),...]
    all_gather x5 -> x0, waiting for transfers between devices: 36.6 us -> none  [the longest x1 20.7 us: shards(): lax.all_gather(tokens, 'seq', axis=0, tiled=True)]
    dot_general x11 -> x0, matrix products: 28.6 us -> none  [the longest x1 6.41 us: shards(): jnp.dot(hidden, lax.all_gather(ffn_down, 'group', axis=1, tiled=True), pr...]
    psum x1 -> x0, waiting for transfers between devices: 13.9 us -> none  [shards(): summed = lax.psum(partial_value, 'seq')]
  transfers between devices with their start and end apart: 7 -> 0, of which waited for: 3 -> 0; matrix products, arithmetic and copies ran while one was open for 14% -> 0% of each run, Pallas kernels for 0% -> 0%
where the time goes in v1:
time: 76.3 us; the launch traced here: 76.1 us
  Pallas kernels  74.2 us (97%)
  local copies, waits for them, and re-layouts  1.87 us (2%)
    pallas_call x1, Pallas kernels, shards(): pl.pallas_call(body, out_shape=jax.ShapeDtypeStruct((2 * HALF, HC), BF),...  74.2 us
    unnamed x1, local copies, waits for them, and re-layouts  1.87 us

profile of v1, /device:TPU:1, one launch (start us, length us, event | category | flops | bytes accessed | tf_op | source)
XLA Modules:
  0.0 76.1 jit_solution(6728335966651092677)
XLA Ops:
  0.0 74.2 %shard_map.100 = bf16[512,512]{1,0:T(8,128)(2,1)} custom-call(bf16[256,1024]{1,0:T(8,128)(2,1)} %tok_h.1, bf16[1024,512]{1,0:T(8,128)(2,1)} %wq_h.1, bf16[1024,512]{1,0:T(8,128)(2,1)} %wk_h.1, bf16[1024,512]{1,0:T(8,128)(2,1)} %wv_h.1, bf16[1024,512]{1,0:T(8,128)(2,1)} %wo_h.1, bf16[64,512]{1,0:T(8,128)(2,1)} %slot_ref.1, f32[1,4]{1,0:T(1,128)} %decay_ref.1, ...), custom_call_target="tpu_custom_call" | custom-call | tf_op jit(solution)/shard_map/pallas_call | solution.py:436
  74.2 1.9 %copy.12 = bf16[512,512]{1,0:T(8,128)(2,1)} copy(bf16[512,512]{1,0:T(8,128)(2,1)} %shard_map.100) | data formatting | bytes 1048576

commit v2 on v1

v2 whole, which is shorter than its diff:
```python
import jax
import jax.numpy as jnp
from jax import lax
from jax.experimental import pallas as pl
from jax.experimental.pallas import tpu as pltpu
from jax.sharding import PartitionSpec as P

HS = 128
MEM = 64
NX, NY, NZ = 4, 4, 8
NG = NX * NY * NZ
HALF = 256
HC = 512
HEADS = 4
D = 1024
PART = MEM // NX
ROWS = HEADS * PART
FS = 512
TAILS = 4
FORWARD = (1, 3, 2)
MESH = pl.DeviceIdType.MESH
F32 = jnp.float32
BF = jnp.bfloat16
FLOOR = -1e30
NULL = 8.0
SCALE = HS ** (-0.5)
LOG2E = 1.4426950408889634


def nn(a, b):
    return lax.dot_general(a, b, (((1,), (0,)), ((), ())), preferred_element_type=F32)


def nt(a, b):
    return lax.dot_general(a, b, (((1,), (1,)), ((), ())), preferred_element_type=F32)


def stat_columns(peak, mass, rate, rows):
    lane = lax.broadcasted_iota(jnp.int32, (rows, 128), 1)
    return jnp.where(lane == 0, peak, jnp.where(lane == 1, mass, jnp.where(lane == 2, rate, 0.0)))


def before_item(items, stop):
    rate = jnp.zeros_like(items[0][0])
    shifted = [None] * len(items)
    for k in reversed(range(len(items))):
        live = k < stop
        shifted[k] = jnp.where(live, items[k][0] - rate, FLOOR)
        rate = rate + jnp.where(live, items[k][2], 0.0)
    peak = shifted[0]
    for a in shifted[1:]:
        peak = jnp.maximum(peak, a)
    weights = [jnp.where(k < stop, jnp.exp(a - peak), 0.0) for k, a in enumerate(shifted)]
    mass = jnp.zeros_like(rate)
    for w, item in zip(weights, items):
        mass = mass + item[1] * w
    return (peak, mass, rate), weights


def weighted(cols, first, values):
    total = cols[:, first : first + 1] * values[0].astype(F32)
    for k in range(1, len(values)):
        total = total + cols[:, first + k : first + k + 1] * values[k].astype(F32)
    return total


def body(
    tok_h, wq_h, wk_h, wv_h, wo_h, slot_ref, decay_ref, up_h, dn_h, gain_ref, out_ref,
    tok, ptok, wq, wk, wv, wo, qs, ks, vs, kp, vp, ff,
    ps, pst, sc, xr, xst, yr, yst, zr, zst, fm, pb, rs, own, pc, pc_in, hid, st, lo, mk, mv, mx,
    tr, relay, load_sem, loc_sem, tok_s, tok_r, tail_s, tail_r, relay_s, relay_r, wx_s, wx_r, rg_s, rg_r, ny_s, ny_r, fy_s, fy_r,
    x_s, x_r, y_s, y_r, z_s, z_r, fm_s, fm_r, rs_s, rs_r, st_s, st_r, mx_s, mx_r,
):
    g = lax.axis_index("group")
    c = lax.axis_index("seq")
    x = lax.rem(g, NX)
    y = lax.rem(g // NX, NY)
    z = g // (NX * NY)
    oc = 1 - c

    def gid(zz, yy, xx):
        return zz * (NX * NY) + yy * NX + xx

    def xp(d):
        return lax.rem(x + d, NX)

    def yp(d):
        return lax.rem(y + d, NY)

    def zp(d):
        return lax.rem(z + d, NZ)

    nxt = lax.rem(g + 1, NG)
    prv = lax.rem(g + NG - 1, NG)
    down_row, up_row = lax.rem(g + NX, NG), lax.rem(g + NG - NX, NG)
    sends = []

    def send(src, dst, ss, rsem, gg, cc):
        cp = pltpu.make_async_remote_copy(
            src_ref=src, dst_ref=dst, send_sem=ss, recv_sem=rsem,
            device_id={"group": gg, "seq": cc}, device_id_type=MESH,
        )
        cp.start()
        sends.append(cp)
        return cp

    def arrived(ref, sem, ss):
        pltpu.make_async_remote_copy(
            src_ref=ref, dst_ref=ref, send_sem=ss, recv_sem=sem,
            device_id={"group": g, "seq": oc}, device_id_type=MESH,
        ).wait_recv()

    loads = []
    for k, (src, dst) in enumerate(
        ((tok_h, tok.at[c]), (wk_h, wk), (wv_h, wv), (wq_h, wq), (wo_h, wo))
    ):
        cp = pltpu.make_async_copy(src, dst, load_sem.at[k])
        cp.start()
        loads.append(cp)
    lanes_x = pl.ds(pl.multiple_of(x * FS, FS), FS)
    wl = []
    for k, (src, dst) in enumerate(((up_h, ff), (dn_h, ff))):
        cp = pltpu.make_async_copy(src.at[:, lanes_x], dst.at[z, y, k, x], loc_sem.at[k])
        cp.start()
        wl.append(cp)

    tr[...] = jnp.zeros_like(tr)
    barrier = pltpu.get_barrier_semaphore()

    def greet(gg, cc):
        pl.semaphore_signal(barrier, inc=1, device_id={"group": gg, "seq": cc}, device_id_type=MESH)

    greet(g, oc)
    for d in range(1, NX):
        greet(gid(z, y, xp(d)), c)
        greet(gid(z, y, xp(d)), oc)
    for d in range(1, NY):
        greet(gid(z, yp(d), x), c)
    for d in range(1, NZ):
        greet(gid(zp(d), y, x), c)
    greet(nxt, c)
    greet(prv, c)
    greet(down_row, c)
    greet(up_row, c)

    def project(half):
        rows = tok[half]
        ks[half] = nn(rows, wk[...]).astype(BF)
        vs[half] = nn(rows, wv[...]).astype(BF)

    pl.semaphore_wait(barrier, 2 * (NX - 1) + (NY - 1) + (NZ - 1) + 5)

    send(tok_h, tok.at[c], tok_s.at[0], tok_r.at[0], g, oc)
    for k, (src, dst) in enumerate(((up_h, ff), (dn_h, ff))):
        for d in range(1, NX):
            to = xp(d)
            send(
                src.at[:, pl.ds(pl.multiple_of(to * FS, FS), FS)], dst.at[z, y, k, x],
                wx_s.at[k, d - 1], wx_r.at[k, d - 1], gid(z, y, to), c,
            )

    row_end, row_start = x == NX - 1, x == 0
    tails, handed, relayed = [], [], []
    for k in range(TAILS):
        rows = slice(k * (HALF // TAILS), (k + 1) * (HALF // TAILS))

        def piece(src, dst, ss, rsem, to):
            return pltpu.make_async_remote_copy(
                src_ref=src, dst_ref=dst, send_sem=ss, recv_sem=rsem,
                device_id={"group": to, "seq": c}, device_id_type=MESH,
            )

        there = ptok.at[c, rows]
        tails.append(piece(tok_h.at[rows], there, tail_s.at[k], tail_r.at[k], nxt))
        handed.append(
            piece(tok_h.at[rows], relay.at[k], tail_s.at[k], relay_r.at[k], gid(z, y, 0))
        )
        relayed.append(piece(relay.at[k], there, relay_s.at[k], tail_r.at[k], down_row))
    sends.extend(tails)

    def tail_start(k, cond):
        pl.when(cond)(tails[k].start)

    def relay_start(k, cond):
        @pl.when(row_start & cond)
        def _():
            handed[k].wait_recv()
            relayed[k].start()

    tail_start(0, x == NX - 1)
    for cp in loads[:3]:
        cp.wait()
    project(c)

    left_y, right_y = yp(NY - 1), yp(1)
    left_z, right_z = zp(NZ - 1), zp(1)

    def weights_x():
        for k in range(2):
            wl[k].wait()
            for d in range(1, NX):
                arrived(ff.at[z, y, k, xp(NX - d)], wx_r.at[k, d - 1], wx_s.at[k, d - 1])

    def weights_ring(step):
        a, b = ff.at[zp(NZ + 1 - step), y], ff.at[zp(step - 1), y]
        if step == NZ // 2:
            a, b = a.at[0], b.at[1]
        send(a, a, rg_s.at[0, step - 1], rg_r.at[0, step - 1], gid(right_z, y, x), c)
        send(b, b, rg_s.at[1, step - 1], rg_r.at[1, step - 1], gid(left_z, y, x), c)

    def ring_wait(step):
        a, b = ff.at[zp(NZ - step), y], ff.at[zp(step), y]
        if step == NZ // 2:
            a, b = a.at[0], b.at[1]
        arrived(a, rg_r.at[0, step - 1], rg_s.at[0, step - 1])
        arrived(b, rg_r.at[1, step - 1], rg_s.at[1, step - 1])

    def weights_near(o):
        b = ff.at[zp(o), y]
        send(b, b, ny_s.at[0, o], ny_r.at[0, o], gid(z, right_y, x), c)
        send(b, b, ny_s.at[1, o], ny_r.at[1, o], gid(z, left_y, x), c)

    def weights_far(o):
        from_left = ff.at[zp(o), left_y]
        from_right = ff.at[zp(o), right_y]
        arrived(from_left, ny_r.at[0, o], ny_s.at[0, o])
        arrived(from_right, ny_r.at[1, o], ny_s.at[1, o])
        if o < NZ // 4:
            src, to = left_y, right_y
        elif o < NZ // 2:
            src = jnp.where(x == 0, right_y, left_y)
            to = jnp.where(x == 0, left_y, right_y)
        else:
            src, to = right_y, left_y
        b = ff.at[zp(o), src]
        send(b, b, fy_s.at[o], fy_r.at[o], gid(z, to, x), c)

    def weights_done():
        for o in range(NZ):
            arrived(ff.at[zp(o), yp(2)], fy_r.at[o], fy_s.at[o])

    arrived(tok.at[oc], tok_r.at[0], tok_s.at[0])
    project(oc)

    for h in range(HEADS):
        cols = slice(h * HS, (h + 1) * HS)
        keys = ks[:, :, cols].reshape(2 * HALF, HS)
        vals = vs[:, :, cols].reshape(2 * HALF, HS)
        scores = nt(slot_ref[:, cols], keys) * SCALE
        peak = jnp.max(scores, axis=1, keepdims=True)
        w = jnp.exp(scores - peak)
        mass = jnp.sum(w, axis=1, keepdims=True)
        pooled = nn(w.astype(BF), vals)
        stat = stat_columns(peak, mass, decay_ref[0:1, h : h + 1], MEM)
        for p in range(NX):
            rows = slice(p * PART, (p + 1) * PART)
            ps[p, h * PART : (h + 1) * PART, :] = pooled[rows].astype(BF)
            first = (p % 2) * ROWS + h * PART
            sc[p // 2, first : first + PART, :] = stat[rows]
    for q in range(2):
        pst[q] = jnp.transpose(sc[q])[0:8]

    for d in range(1, NX):
        to = xp(d)
        send(ps.at[to], xr.at[x], x_s.at[0, d - 1], x_r.at[0, d - 1], gid(z, y, to), c)
        send(pst.at[to // 2], xst.at[x], x_s.at[1, d - 1], x_r.at[1, d - 1], gid(z, y, to), c)
    for k in range(TAILS):
        tail_start(k, x < NX - 1)
        if k:
            pl.when(row_end)(handed[k].start)
    xr[x] = ps[x]
    xst[x] = pst[x // 2]
    weights_x()
    weights_ring(1)
    weights_near(0)
    loads[3].wait()
    for half in range(2):
        qs[half] = nn(tok[half], wq[...]).astype(BF)
    for d in range(1, NX):
        frm = xp(NX - d)
        arrived(xr.at[frm], x_r.at[0, d - 1], x_s.at[0, d - 1])
        arrived(xst.at[frm], x_r.at[1, d - 1], x_s.at[1, d - 1])
    odd = lax.rem(x, 2) == 1
    items = []
    for k in range(NX):
        tile = xst[k]
        tile = jnp.where(odd, pltpu.roll(tile, 64, 1), tile)
        items.append(tuple(tile[r : r + 1] for r in range(3)))
    in_row = [before_item(items, j) for j in range(NX + 1)]
    n = 0
    for j in range(1, NX + 1):
        for k in range(j):
            tr[n : n + 1] = in_row[j][1][k]
            n += 1
    cols = jnp.transpose(tr[...])[0:ROWS]
    row_val = [None]
    n = 0
    for j in range(1, NX + 1):
        row_val.append(weighted(cols, n, [xr[k] for k in range(j)]))
        n += j

    def stat_tile(state):
        sub = lax.broadcasted_iota(jnp.int32, (8, 128), 0)
        return jnp.where(sub == 0, state[0], jnp.where(sub == 1, state[1], state[2]))

    yr[y] = row_val[NX].astype(BF)
    yst[y] = stat_tile(in_row[NX][0])
    for d in range(1, NY):
        to = gid(z, yp(d), x)
        send(yr.at[y], yr.at[y], y_s.at[0, d - 1], y_r.at[0, d - 1], to, c)
        send(yst.at[y], yst.at[y], y_s.at[1, d - 1], y_r.at[1, d - 1], to, c)
    ring_wait(1)
    weights_ring(2)
    weights_near(1)
    weights_near(NZ - 1)
    for d in range(1, NY):
        frm = yp(NY - d)
        arrived(yr.at[frm], y_r.at[0, d - 1], y_s.at[0, d - 1])
        arrived(yst.at[frm], y_r.at[1, d - 1], y_s.at[1, d - 1])
    items = [tuple(yst[k, r : r + 1] for r in range(3)) for k in range(NY)]
    in_plane, w_some = before_item(items, y)
    plane, w_all = before_item(items, NY)
    for k in range(NY):
        tr[k : k + 1] = w_all[k]
        tr[NY + k : NY + k + 1] = w_some[k]
    cols = jnp.transpose(tr[...])[0:ROWS]
    vals = [yr[k] for k in range(NY)]

    zr[z] = weighted(cols, 0, vals).astype(BF)
    zst[z] = stat_tile(plane)
    for d in range(1, NZ):
        to = gid(zp(d), y, x)
        send(zr.at[z], zr.at[z], z_s.at[0, d - 1], z_r.at[0, d - 1], to, c)
        send(zst.at[z], zst.at[z], z_s.at[1, d - 1], z_r.at[1, d - 1], to, c)
    plane_val = weighted(cols, NY, vals)
    ring_wait(2)
    weights_ring(3)
    weights_near(2)
    weights_near(NZ - 2)
    weights_far(0)
    weights_far(1)
    weights_far(NZ - 1)
    relay_start(1, y < NY - 1)
    for d in range(1, NZ):
        frm = zp(NZ - d)
        arrived(zr.at[frm], z_r.at[0, d - 1], z_s.at[0, d - 1])
        arrived(zst.at[frm], z_r.at[1, d - 1], z_s.at[1, d - 1])
    items = [tuple(zst[k, r : r + 1] for r in range(3)) for k in range(NZ)]
    planes, w_some = before_item(items, z)
    for k in range(NZ):
        tr[k : k + 1] = w_some[k]
    n = NZ
    for j in range(NX):
        own_peak, own_mass, own_rate = in_row[j][0]
        shifted = [planes[0] - in_plane[2] - own_rate, in_plane[0] - own_rate, own_peak]
        peak = jnp.maximum(jnp.maximum(shifted[0], shifted[1]), shifted[2])
        parts = [jnp.exp(a - peak) for a in shifted]
        mass = planes[1] * parts[0] + in_plane[1] * parts[1] + own_mass * parts[2]
        anchor = jnp.maximum(peak, NULL)
        factor = jnp.exp(peak - anchor)
        coef = factor / (mass * factor + jnp.exp(NULL - anchor))
        for part in parts:
            tr[n : n + 1] = part * coef
            n += 1
    cols = jnp.transpose(tr[...])[0:ROWS]
    planes_val = weighted(cols, 0, [zr[k] for k in range(NZ)])
    for j in range(NX):
        vals = [planes_val, plane_val] + ([row_val[j]] if j else [])
        memory = weighted(cols, NZ + 3 * j, vals).astype(BF)
        for h in range(HEADS):
            fm[c, x, j * PART : (j + 1) * PART, h * HS : (h + 1) * HS] = memory[
                h * PART : (h + 1) * PART
            ]
    b = fm.at[c, x]
    for d in range(1, NX):
        send(b, b, fm_s.at[0, d], fm_r.at[0, d], gid(z, y, xp(d)), c)
    send(b, b, fm_s.at[1, 0], fm_r.at[1, 0], g, oc)
    weights_far(2)
    weights_far(NZ - 2)
    ring_wait(3)
    weights_ring(4)
    weights_near(3)
    weights_near(NZ - 3)
    relay_start(1, y == NY - 1)
    ring_wait(NZ // 2)
    weights_near(NZ // 2)
    for d in FORWARD:
        b = fm.at[c, xp(NX - d)]
        arrived(b, fm_r.at[0, d], fm_s.at[0, d])
        send(b, b, fm_s.at[1, d], fm_r.at[1, d], g, oc)
    weights_far(3)
    weights_far(NZ - 3)
    weights_far(NZ // 2)
    relay_start(2, True)
    relay_start(3, True)
    arrived(fm.at[oc, x], fm_r.at[1, 0], fm_s.at[1, 0])
    for d in FORWARD:
        arrived(fm.at[oc, xp(NX - d)], fm_r.at[1, d], fm_s.at[1, d])
    weights_done()
    up = ff[:, :, 0].reshape(D, FS)
    total = nn(fm[0].reshape(NX * MEM, HC), up[0:HC]) + nn(fm[1].reshape(NX * MEM, HC), up[HC:])
    hid[...] = jax.nn.gelu(total, approximate=True).astype(BF).reshape(2, 2 * MEM, FS)
    down = ff[:, :, 1].reshape(D, FS)
    pc[...] = nt(hid[oc], down).astype(BF)
    send(pc, pc_in, rs_s.at[0], rs_r.at[0], g, oc)
    own[...] = nt(hid[c], down)
    arrived(pc_in, rs_r.at[0], rs_s.at[0])
    own[...] += pc_in[...].astype(F32)
    for j in range(NX):
        for q in range(2):
            first = q * MEM + j * PART
            pb[j, q * PART : (q + 1) * PART, :] = own[first : first + PART].astype(BF)
    for d in FORWARD:
        to = xp(d)
        send(pb.at[to], rs.at[d - 1], rs_s.at[d], rs_r.at[d], gid(z, y, to), c)
    for cp in tails:
        cp.wait_recv()
    send(ptok.at[c], ptok.at[c], tok_s.at[1], tok_r.at[1], g, oc)

    def project_prev(half):
        rows = ptok[half]
        kp[half] = nn(rows, wk[...]).astype(BF)
        vp[half] = nn(rows, wv[...]).astype(BF)

    project_prev(c)
    arrived(ptok.at[oc], tok_r.at[1], tok_s.at[1])
    project_prev(oc)

    row_i = lax.broadcasted_iota(jnp.int32, (HALF, HALF), 0)
    col_i = lax.broadcasted_iota(jnp.int32, (HALF, HALF), 1)
    tri = col_i <= row_i
    bias = jnp.where(g == 0, FLOOR, 0.0).astype(F32)

    def attend(h, i):
        cols = slice(h * HS, (h + 1) * HS)
        q = qs[i, :, cols]
        near = nt(q, ks[i, :, cols])
        far = nt(q, kp[i, :, cols]) + bias
        diag = jnp.where(tri, near, far)
        if i == 0:
            full = nt(q, kp[1, :, cols]) + bias
            full_v = vp[1, :, cols]
        else:
            full = nt(q, ks[0, :, cols])
            full_v = vs[0, :, cols]
        high = jnp.maximum(
            jnp.max(diag, axis=1, keepdims=True), jnp.max(full, axis=1, keepdims=True)
        )
        ed = jnp.exp2((diag - high) * (SCALE * LOG2E))
        ef = jnp.exp2((full - high) * (SCALE * LOG2E))
        mass = jnp.sum(ed, axis=1, keepdims=True) + jnp.sum(ef, axis=1, keepdims=True)
        acc = nn(jnp.where(tri, ed, 0.0).astype(BF), vs[i, :, cols])
        acc += nn(jnp.where(tri, 0.0, ed).astype(BF), vp[i, :, cols])
        acc += nn(ef.astype(BF), full_v)
        lo[i, :, cols] = acc / mass

    for h in range(HEADS):
        for i in range(2):
            attend(h, i)
    for d in FORWARD:
        arrived(rs.at[d - 1], rs_r.at[d], rs_s.at[d])
    mine = pl.ds(pl.multiple_of(x * PART, PART), PART)
    acc = jnp.concatenate(
        [own[pl.ds(pl.multiple_of(q * MEM + x * PART, PART), PART), :] for q in range(2)], 0
    )
    mem = fm[:, pl.ds(2 * c, 2), mine, :]
    mem = jnp.concatenate(
        [mem[0].reshape(2 * PART, HC), mem[1].reshape(2 * PART, HC)], 1
    ).astype(F32)
    for d in range(NX - 1):
        acc += rs[d].astype(F32)
    summed = mem + acc
    scaled = summed * lax.rsqrt(jnp.mean(summed * summed, axis=-1, keepdims=True) + 1e-06)
    st[c] = (scaled * gain_ref[...]).astype(BF)
    send(st.at[c], st.at[c], st_s, st_r, g, oc)
    arrived(st.at[oc], st_r, st_s)
    settled = st[...].reshape(MEM, D)
    mk[...] = nn(settled, wk[...]).astype(BF)
    mv[...] = nn(settled, wv[...]).astype(BF)

    loads[4].wait()
    def out_part(cc, h):
        return nn(mx[cc, h], wo[pl.ds(pl.multiple_of(cc * HC + h * HS, HS), HS), :])

    for h in range(HEADS):
        cols = slice(h * HS, (h + 1) * HS)
        q = qs[:, :, cols].reshape(2 * HALF, HS)
        scores = nt(q, mk[:, cols])
        high = jnp.max(scores, axis=1, keepdims=True)
        e = jnp.exp2((scores - high) * (SCALE * LOG2E))
        probs = (e / jnp.sum(e, axis=1, keepdims=True)).astype(BF)
        cross = nn(probs, mv[:, cols])
        both = lo[:, :, cols].reshape(2 * HALF, HS) + cross
        mx[c, h] = both.astype(BF)
        send(mx.at[c, h], mx.at[c, h], mx_s.at[h], mx_r.at[h], g, oc)
    acc = out_part(c, 0)
    for h in range(1, HEADS):
        acc += out_part(c, h)
    for h in range(HEADS):
        arrived(mx.at[oc, h], mx_r.at[h], mx_s.at[h])
        acc += out_part(oc, h)
    out_ref[...] = acc.astype(BF)

    for cp in sends:
        cp.wait_send()
    for k in range(1, TAILS):
        pl.when(row_start)(relayed[k].wait_send)


def shards(tokens, w_query, w_key, w_value, w_out, slot_query, span_decay, ffn_up, ffn_down, norm_gain):
    V = pltpu.VMEM
    DMA = pltpu.SemaphoreType.DMA
    scratch = [
        V((2, HALF, D), BF), V((2, HALF, D), BF),
        V((D, HC), BF), V((D, HC), BF), V((D, HC), BF), V((D, HC), BF),
        V((2, HALF, HC), BF), V((2, HALF, HC), BF), V((2, HALF, HC), BF),
        V((2, HALF, HC), BF), V((2, HALF, HC), BF),
        V((NZ, NY, 2, NX, 8, FS), BF),
        V((NX, ROWS, HS), BF), V((2, 8, 128), F32), V((2, 128, 128), F32),
        V((NX, ROWS, HS), BF), V((NX, 8, 128), F32),
        V((NY, ROWS, HS), BF), V((NY, 8, 128), F32),
        V((NZ, ROWS, HS), BF), V((NZ, 8, 128), F32),
        V((2, NX, NX * PART, HC), BF),
        V((NX, 2 * PART, D), BF), V((NX - 1, 2 * PART, D), BF), V((2 * MEM, D), F32),
        V((2 * MEM, D), BF), V((2 * MEM, D), BF), V((2, 2 * MEM, FS), BF),
        V((2, 2 * PART, D), BF),
        V((2, HALF, HC), F32),
        V((MEM, HC), BF), V((MEM, HC), BF),
        V((2, HEADS, 2 * HALF, HS), BF),
        V((128, 128), F32), V((TAILS, HALF // TAILS, D), BF),
        DMA((5,)), DMA((2,)), DMA((2,)), DMA((2,)), DMA((TAILS,)), DMA((TAILS,)), DMA((TAILS,)), DMA((TAILS,)),
        DMA((2, NX - 1)), DMA((2, NX - 1)), DMA((2, NZ // 2)), DMA((2, NZ // 2)),
        DMA((2, NZ)), DMA((2, NZ)), DMA((NZ,)), DMA((NZ,)),
        DMA((2, NX - 1)), DMA((2, NX - 1)), DMA((2, NY - 1)), DMA((2, NY - 1)),
        DMA((2, NZ - 1)), DMA((2, NZ - 1)),
        DMA((2, NX)), DMA((2, NX)), DMA((NX,)), DMA((NX,)), DMA, DMA, DMA((HEADS,)), DMA((HEADS,)),
    ]
    args = (
        tokens, w_query, w_key, w_value, w_out, slot_query, span_decay, ffn_up,
        ffn_down.T, norm_gain.reshape(1, D),
    )
    hbm = pl.BlockSpec(memory_space=pltpu.HBM)
    vm = pl.BlockSpec(memory_space=pltpu.VMEM)
    return pl.pallas_call(
        body,
        out_shape=jax.ShapeDtypeStruct((2 * HALF, HC), BF),
        in_specs=[hbm, hbm, hbm, hbm, hbm, vm, vm, hbm, hbm, vm],
        out_specs=vm,
        scratch_shapes=scratch,
        compiler_params=pltpu.CompilerParams(
            collective_id=0, has_side_effects=True, vmem_limit_bytes=48 * 1024 * 1024
        ),
    )(*[pltpu.with_memory_space_constraint(a, pltpu.HBM) for a in args])


def solution(mesh):
    in_specs = (
        P(("group", "seq"), None),
        P(None, "seq"),
        P(None, "seq"),
        P(None, "seq"),
        P(None, "seq"),
        P(None, "seq"),
        P("group", "seq"),
        P("group", "seq"),
        P("seq", "group"),
        P(),
    )
    out_specs = P("group", "seq")
    return jax.shard_map(shards, mesh=mesh, in_specs=in_specs, out_specs=out_specs, check_vma=False)
```

time: 76.3 us -> 60.8 us (0.80)
  Pallas kernels: 74.2 us -> 59.9 us
  local copies, waits for them, and re-layouts: 1.87 us -> 0.8 us
    pallas_call x1, Pallas kernels: 74.2 us -> 59.9 us  [shards(): pl.pallas_call(body, out_shape=jax.ShapeDtypeStruct((2 * HALF, HC), BF),...]
    unnamed x1, local copies, waits for them, and re-layouts: 1.87 us -> 0.8 us
where the time goes in v2:
time: 60.8 us; the launch traced here: 60.7 us
  Pallas kernels  59.9 us (99%)
  local copies, waits for them, and re-layouts  0.8 us (1%)
    pallas_call x1, Pallas kernels, shards(): pl.pallas_call(body, out_shape=jax.ShapeDtypeStruct((2 * HALF, HC), BF),...  59.9 us

profile of v2, /device:TPU:1, one launch (start us, length us, event | category | flops | bytes accessed | tf_op | source)
XLA Modules:
  0.0 60.7 jit_solution(5962921926130856697)
XLA Ops:
  0.0 59.9 %shard_map.100 = bf16[512,512]{1,0:T(8,128)(2,1)S(1)} custom-call(bf16[256,1024]{1,0:T(8,128)(2,1)} %tok_h.1, bf16[1024,512]{1,0:T(8,128)(2,1)} %wq_h.1, bf16[1024,512]{1,0:T(8,128)(2,1)} %wk_h.1, bf16[1024,512]{1,0:T(8,128)(2,1)} %wv_h.1, bf16[1024,512]{1,0:T(8,128)(2,1)} %wo_h.1, bf16[64,512]{1,0:T(8,128)(2,1)} %slot_ref.1, f32[1,4]{1,0:T(1,128)} %decay_ref.1, ...), custom_call_target="tpu_custom_call" | custom-call | tf_op jit(solution)/shard_map/pallas_call | solution.py:544
  59.9 0.8 %copy.12 = bf16[512,512]{1,0:T(8,128)(2,1)} copy(bf16[512,512]{1,0:T(8,128)(2,1)S(1)} %shard_map.100) | data formatting | bytes 1048576

commit v3 on v2

--- a/solution.py
+++ b/solution.py
@@ -65,8 +65,8 @@
 
 
 def body(
-    tok_h, wq_h, wk_h, wv_h, wo_h, slot_ref, decay_ref, up_h, dn_h, gain_ref, out_ref,
-    tok, ptok, wq, wk, wv, wo, qs, ks, vs, kp, vp, ff,
+    tok_h, wq_h, wk_h, wv_h, wo_h, slot_h, decay_h, up_h, dn_h, gain_h, out_ref,
+    tok, ptok, wq, wk, wv, wo, slot_ref, decay_ref, gain_ref, qs, ks, vs, kp, vp, ff,
     ps, pst, sc, xr, xst, yr, yst, zr, zst, fm, pb, rs, own, pc, pc_in, hid, st, lo, mk, mv, mx,
     tr, relay, load_sem, loc_sem, tok_s, tok_r, tail_s, tail_r, relay_s, relay_r, wx_s, wx_r, rg_s, rg_r, ny_s, ny_r, fy_s, fy_r,
     x_s, x_r, y_s, y_r, z_s, z_r, fm_s, fm_r, rs_s, rs_r, st_s, st_r, mx_s, mx_r,
@@ -109,20 +109,6 @@
             src_ref=ref, dst_ref=ref, send_sem=ss, recv_sem=sem,
             device_id={"group": g, "seq": oc}, device_id_type=MESH,
         ).wait_recv()
-
-    loads = []
-    for k, (src, dst) in enumerate(
-        ((tok_h, tok.at[c]), (wk_h, wk), (wv_h, wv), (wq_h, wq), (wo_h, wo))
-    ):
-        cp = pltpu.make_async_copy(src, dst, load_sem.at[k])
-        cp.start()
-        loads.append(cp)
-    lanes_x = pl.ds(pl.multiple_of(x * FS, FS), FS)
-    wl = []
-    for k, (src, dst) in enumerate(((up_h, ff), (dn_h, ff))):
-        cp = pltpu.make_async_copy(src.at[:, lanes_x], dst.at[z, y, k, x], loc_sem.at[k])
-        cp.start()
-        wl.append(cp)
 
     tr[...] = jnp.zeros_like(tr)
     barrier = pltpu.get_barrier_semaphore()
@@ -143,6 +129,23 @@
     greet(down_row, c)
     greet(up_row, c)
 
+    loads = []
+    for k, (src, dst) in enumerate(
+        (
+            (tok_h, tok.at[c]), (wk_h, wk), (wv_h, wv), (wq_h, wq), (wo_h, wo),
+            (slot_h, slot_ref), (decay_h, decay_ref), (gain_h, gain_ref),
+        )
+    ):
+        cp = pltpu.make_async_copy(src, dst, load_sem.at[k])
+        cp.start()
+        loads.append(cp)
+    lanes_x = pl.ds(pl.multiple_of(x * FS, FS), FS)
+    wl = []
+    for k, (src, dst) in enumerate(((up_h, ff), (dn_h, ff))):
+        cp = pltpu.make_async_copy(src.at[:, lanes_x], dst.at[z, y, k, x], loc_sem.at[k])
+        cp.start()
+        wl.append(cp)
+
     def project(half):
         rows = tok[half]
         ks[half] = nn(rows, wk[...]).astype(BF)
@@ -159,7 +162,9 @@
                 wx_s.at[k, d - 1], wx_r.at[k, d - 1], gid(z, y, to), c,
             )
 
-    row_end, row_start = x == NX - 1, x == 0
+    row_end = (x == NX - 1) & (g < NG - 1)
+    row_start = (x == 0) & (g < NG - NX)
+    follows = g > 0
     tails, handed, relayed = [], [], []
     for k in range(TAILS):
         rows = slice(k * (HALF // TAILS), (k + 1) * (HALF // TAILS))
@@ -176,7 +181,6 @@
             piece(tok_h.at[rows], relay.at[k], tail_s.at[k], relay_r.at[k], gid(z, y, 0))
         )
         relayed.append(piece(relay.at[k], there, relay_s.at[k], tail_r.at[k], down_row))
-    sends.extend(tails)
 
     def tail_start(k, cond):
         pl.when(cond)(tails[k].start)
@@ -187,7 +191,7 @@
             handed[k].wait_recv()
             relayed[k].start()
 
-    tail_start(0, x == NX - 1)
+    tail_start(0, row_end)
     for cp in loads[:3]:
         cp.wait()
     project(c)
@@ -242,6 +246,8 @@
     arrived(tok.at[oc], tok_r.at[0], tok_s.at[0])
     project(oc)
 
+    loads[5].wait()
+    loads[6].wait()
     for h in range(HEADS):
         cols = slice(h * HS, (h + 1) * HS)
         keys = ks[:, :, cols].reshape(2 * HALF, HS)
@@ -384,15 +390,42 @@
     relay_start(1, y == NY - 1)
     ring_wait(NZ // 2)
     weights_near(NZ // 2)
+    quarter = HALF // 2
+    parts = [slice(j * quarter, (j + 1) * quarter) for j in range(2)]
+    across = [
+        pltpu.make_async_remote_copy(
+            src_ref=ptok.at[c, r], dst_ref=ptok.at[c, r], send_sem=tok_s.at[1 + j],
+            recv_sem=tok_r.at[1 + j], device_id={"group": g, "seq": oc}, device_id_type=MESH,
+        )
+        for j, r in enumerate(parts)
+    ]
+
+    def project_prev(half, r):
+        rows = ptok[half, r]
+        kp[half, r] = nn(rows, wk[...]).astype(BF)
+        vp[half, r] = nn(rows, wv[...]).astype(BF)
+
+    def prev_take(j):
+        for k in range(j * TAILS // 2, (j + 1) * TAILS // 2):
+            tails[k].wait_recv()
+        across[j].start()
+        project_prev(c, parts[j])
+
+    def prev_rest(j):
+        arrived(ptok.at[oc, parts[j]], tok_r.at[1 + j], tok_s.at[1 + j])
+        project_prev(oc, parts[j])
+
     for d in FORWARD:
         b = fm.at[c, xp(NX - d)]
         arrived(b, fm_r.at[0, d], fm_s.at[0, d])
         send(b, b, fm_s.at[1, d], fm_r.at[1, d], g, oc)
+    pl.when(follows)(lambda: prev_take(0))
     weights_far(3)
     weights_far(NZ - 3)
     weights_far(NZ // 2)
     relay_start(2, True)
     relay_start(3, True)
+    pl.when(follows)(lambda: prev_rest(0))
     arrived(fm.at[oc, x], fm_r.at[1, 0], fm_s.at[1, 0])
     for d in FORWARD:
         arrived(fm.at[oc, xp(NX - d)], fm_r.at[1, d], fm_s.at[1, d])
@@ -413,18 +446,15 @@
     for d in FORWARD:
         to = xp(d)
         send(pb.at[to], rs.at[d - 1], rs_s.at[d], rs_r.at[d], gid(z, y, to), c)
-    for cp in tails:
-        cp.wait_recv()
-    send(ptok.at[c], ptok.at[c], tok_s.at[1], tok_r.at[1], g, oc)
-
-    def project_prev(half):
-        rows = ptok[half]
-        kp[half] = nn(rows, wk[...]).astype(BF)
-        vp[half] = nn(rows, wv[...]).astype(BF)
-
-    project_prev(c)
-    arrived(ptok.at[oc], tok_r.at[1], tok_s.at[1])
-    project_prev(oc)
+    @pl.when(follows)
+    def _():
+        prev_take(1)
+        prev_rest(1)
+
+    @pl.when(g == 0)
+    def _():
+        kp[...] = jnp.zeros_like(kp)
+        vp[...] = jnp.zeros_like(vp)
 
     row_i = lax.broadcasted_iota(jnp.int32, (HALF, HALF), 0)
     col_i = lax.broadcasted_iota(jnp.int32, (HALF, HALF), 1)
@@ -457,6 +487,8 @@
     for h in range(HEADS):
         for i in range(2):
             attend(h, i)
+    loads[4].wait()
+    loads[7].wait()
     for d in FORWARD:
         arrived(rs.at[d - 1], rs_r.at[d], rs_s.at[d])
     mine = pl.ds(pl.multiple_of(x * PART, PART), PART)
@@ -478,7 +510,6 @@
     mk[...] = nn(settled, wk[...]).astype(BF)
     mv[...] = nn(settled, wv[...]).astype(BF)
 
-    loads[4].wait()
     def out_part(cc, h):
         return nn(mx[cc, h], wo[pl.ds(pl.multiple_of(cc * HC + h * HS, HS), HS), :])
 
@@ -503,8 +534,12 @@
 
     for cp in sends:
         cp.wait_send()
-    for k in range(1, TAILS):
-        pl.when(row_start)(relayed[k].wait_send)
+    for k in range(TAILS):
+        pl.when(g < NG - 1)(tails[k].wait_send)
+        if k:
+            pl.when(row_start)(relayed[k].wait_send)
+    for cp in across:
+        pl.when(follows)(cp.wait_send)
 
 
 def shards(tokens, w_query, w_key, w_value, w_out, slot_query, span_decay, ffn_up, ffn_down, norm_gain):
@@ -513,6 +548,7 @@
     scratch = [
         V((2, HALF, D), BF), V((2, HALF, D), BF),
         V((D, HC), BF), V((D, HC), BF), V((D, HC), BF), V((D, HC), BF),
+        V((MEM, HC), BF), V((1, HEADS), F32), V((1, D), F32),
         V((2, HALF, HC), BF), V((2, HALF, HC), BF), V((2, HALF, HC), BF),
         V((2, HALF, HC), BF), V((2, HALF, HC), BF),
         V((NZ, NY, 2, NX, 8, FS), BF),
@@ -528,7 +564,7 @@
         V((MEM, HC), BF), V((MEM, HC), BF),
         V((2, HEADS, 2 * HALF, HS), BF),
         V((128, 128), F32), V((TAILS, HALF // TAILS, D), BF),
-        DMA((5,)), DMA((2,)), DMA((2,)), DMA((2,)), DMA((TAILS,)), DMA((TAILS,)), DMA((TAILS,)), DMA((TAILS,)),
+        DMA((8,)), DMA((2,)), DMA((3,)), DMA((3,)), DMA((TAILS,)), DMA((TAILS,)), DMA((TAILS,)), DMA((TAILS,)),
         DMA((2, NX - 1)), DMA((2, NX - 1)), DMA((2, NZ // 2)), DMA((2, NZ // 2)),
         DMA((2, NZ)), DMA((2, NZ)), DMA((NZ,)), DMA((NZ,)),
         DMA((2, NX - 1)), DMA((2, NX - 1)), DMA((2, NY - 1)), DMA((2, NY - 1)),
@@ -544,7 +580,7 @@
     return pl.pallas_call(
         body,
         out_shape=jax.ShapeDtypeStruct((2 * HALF, HC), BF),
-        in_specs=[hbm, hbm, hbm, hbm, hbm, vm, vm, hbm, hbm, vm],
+        in_specs=[hbm] * 10,
         out_specs=vm,
         scratch_shapes=scratch,
         compiler_params=pltpu.CompilerParams(

time: 60.8 us -> 57 us (0.938)
  the two profiles are of different devices: /device:TPU:1 before, /device:TPU:105 now
where the time goes in v3:
time: 57 us
  Pallas kernels  56.2 us (99%)
  local copies, waits for them, and re-layouts  0.8 us (1%)
    pallas_call x1, Pallas kernels, shards(): pl.pallas_call(body, out_shape=jax.ShapeDtypeStruct((2 * HALF, HC), BF),...  56.2 us

profile of v3, /device:TPU:105, one launch (start us, length us, event | category | flops | bytes accessed | tf_op | source)
XLA Modules:
  0.0 57.0 jit_solution(151846194551652966)
XLA Ops:
  0.0 56.2 %shard_map.100 = bf16[512,512]{1,0:T(8,128)(2,1)S(1)} custom-call(bf16[256,1024]{1,0:T(8,128)(2,1)} %tok_h.1, bf16[1024,512]{1,0:T(8,128)(2,1)} %wq_h.1, bf16[1024,512]{1,0:T(8,128)(2,1)} %wk_h.1, bf16[1024,512]{1,0:T(8,128)(2,1)} %wv_h.1, bf16[1024,512]{1,0:T(8,128)(2,1)} %wo_h.1, bf16[64,512]{1,0:T(8,128)(2,1)} %slot_h.1, f32[1,4]{1,0:T(1,128)} %decay_h.1, ...), custom_call_target="tpu_custom_call" | custom-call | tf_op jit(solution)/shard_map/pallas_call | solution.py:580
  56.2 0.8 %copy.12 = bf16[512,512]{1,0:T(8,128)(2,1)} copy(bf16[512,512]{1,0:T(8,128)(2,1)S(1)} %shard_map.100) | data formatting | bytes 1048576

commit v4 on v3

--- a/solution.py
+++ b/solution.py
@@ -69,7 +69,7 @@
     tok, ptok, wq, wk, wv, wo, slot_ref, decay_ref, gain_ref, qs, ks, vs, kp, vp, ff,
     ps, pst, sc, xr, xst, yr, yst, zr, zst, fm, pb, rs, own, pc, pc_in, hid, st, lo, mk, mv, mx,
     tr, relay, load_sem, loc_sem, tok_s, tok_r, tail_s, tail_r, relay_s, relay_r, wx_s, wx_r, rg_s, rg_r, ny_s, ny_r, fy_s, fy_r,
-    x_s, x_r, y_s, y_r, z_s, z_r, fm_s, fm_r, rs_s, rs_r, st_s, st_r, mx_s, mx_r,
+    x_s, x_r, y_s, y_r, z_s, z_r, fm_s, fm_r, pc_s, pc_r, rs_s, rs_r, st_s, st_r, mx_s, mx_r,
 ):
     g = lax.axis_index("group")
     c = lax.axis_index("seq")
@@ -205,43 +205,48 @@
             for d in range(1, NX):
                 arrived(ff.at[z, y, k, xp(NX - d)], wx_r.at[k, d - 1], wx_s.at[k, d - 1])
 
-    def weights_ring(step):
-        a, b = ff.at[zp(NZ + 1 - step), y], ff.at[zp(step - 1), y]
+    def weights_ring(step, row=y, lane=0):
+        a, b = ff.at[zp(NZ + 1 - step), row], ff.at[zp(step - 1), row]
         if step == NZ // 2:
             a, b = a.at[0], b.at[1]
-        send(a, a, rg_s.at[0, step - 1], rg_r.at[0, step - 1], gid(right_z, y, x), c)
-        send(b, b, rg_s.at[1, step - 1], rg_r.at[1, step - 1], gid(left_z, y, x), c)
-
-    def ring_wait(step):
-        a, b = ff.at[zp(NZ - step), y], ff.at[zp(step), y]
+        k = step - 1
+        send(a, a, rg_s.at[lane, 0, k], rg_r.at[lane, 0, k], gid(right_z, y, x), c)
+        send(b, b, rg_s.at[lane, 1, k], rg_r.at[lane, 1, k], gid(left_z, y, x), c)
+
+    def ring_wait(step, row=y, lane=0):
+        a, b = ff.at[zp(NZ - step), row], ff.at[zp(step), row]
         if step == NZ // 2:
             a, b = a.at[0], b.at[1]
-        arrived(a, rg_r.at[0, step - 1], rg_s.at[0, step - 1])
-        arrived(b, rg_r.at[1, step - 1], rg_s.at[1, step - 1])
+        arrived(a, rg_r.at[lane, 0, step - 1], rg_s.at[lane, 0, step - 1])
+        arrived(b, rg_r.at[lane, 1, step - 1], rg_s.at[lane, 1, step - 1])
+
+    far_y = yp(2)
+
+    def far_ring(step):
+        if step == 1:
+            arrived(ff.at[z, far_y], fy_r, fy_s)
+        else:
+            ring_wait(step - 1, far_y, 1)
+        weights_ring(step, far_y, 1)
 
     def weights_near(o):
         b = ff.at[zp(o), y]
         send(b, b, ny_s.at[0, o], ny_r.at[0, o], gid(z, right_y, x), c)
         send(b, b, ny_s.at[1, o], ny_r.at[1, o], gid(z, left_y, x), c)
 
-    def weights_far(o):
-        from_left = ff.at[zp(o), left_y]
-        from_right = ff.at[zp(o), right_y]
-        arrived(from_left, ny_r.at[0, o], ny_s.at[0, o])
-        arrived(from_right, ny_r.at[1, o], ny_s.at[1, o])
-        if o < NZ // 4:
-            src, to = left_y, right_y
-        elif o < NZ // 2:
-            src = jnp.where(x == 0, right_y, left_y)
-            to = jnp.where(x == 0, left_y, right_y)
-        else:
-            src, to = right_y, left_y
-        b = ff.at[zp(o), src]
-        send(b, b, fy_s.at[o], fy_r.at[o], gid(z, to, x), c)
+    def near_wait(o):
+        arrived(ff.at[zp(o), left_y], ny_r.at[0, o], ny_s.at[0, o])
+        arrived(ff.at[zp(o), right_y], ny_r.at[1, o], ny_s.at[1, o])
+
+    def weights_far():
+        near_wait(0)
+        b = ff.at[z, left_y]
+        send(b, b, fy_s, fy_r, gid(z, right_y, x), c)
 
     def weights_done():
-        for o in range(NZ):
-            arrived(ff.at[zp(o), yp(2)], fy_r.at[o], fy_s.at[o])
+        for o in range(1, NZ):
+            near_wait(o)
+        ring_wait(NZ // 2, far_y, 1)
 
     arrived(tok.at[oc], tok_r.at[0], tok_s.at[0])
     project(oc)
@@ -317,6 +322,7 @@
         send(yst.at[y], yst.at[y], y_s.at[1, d - 1], y_r.at[1, d - 1], to, c)
     ring_wait(1)
     weights_ring(2)
+    weights_far()
     weights_near(1)
     weights_near(NZ - 1)
     for d in range(1, NY):
@@ -339,13 +345,11 @@
         send(zr.at[z], zr.at[z], z_s.at[0, d - 1], z_r.at[0, d - 1], to, c)
         send(zst.at[z], zst.at[z], z_s.at[1, d - 1], z_r.at[1, d - 1], to, c)
     plane_val = weighted(cols, NY, vals)
+    far_ring(1)
     ring_wait(2)
     weights_ring(3)
     weights_near(2)
     weights_near(NZ - 2)
-    weights_far(0)
-    weights_far(1)
-    weights_far(NZ - 1)
     relay_start(1, y < NY - 1)
     for d in range(1, NZ):
         frm = zp(NZ - d)
@@ -381,8 +385,7 @@
     for d in range(1, NX):
         send(b, b, fm_s.at[0, d], fm_r.at[0, d], gid(z, y, xp(d)), c)
     send(b, b, fm_s.at[1, 0], fm_r.at[1, 0], g, oc)
-    weights_far(2)
-    weights_far(NZ - 2)
+    far_ring(2)
     ring_wait(3)
     weights_ring(4)
     weights_near(3)
@@ -390,6 +393,7 @@
     relay_start(1, y == NY - 1)
     ring_wait(NZ // 2)
     weights_near(NZ // 2)
+    far_ring(3)
     quarter = HALF // 2
     parts = [slice(j * quarter, (j + 1) * quarter) for j in range(2)]
     across = [
@@ -420,9 +424,7 @@
         arrived(b, fm_r.at[0, d], fm_s.at[0, d])
         send(b, b, fm_s.at[1, d], fm_r.at[1, d], g, oc)
     pl.when(follows)(lambda: prev_take(0))
-    weights_far(3)
-    weights_far(NZ - 3)
-    weights_far(NZ // 2)
+    far_ring(NZ // 2)
     relay_start(2, True)
     relay_start(3, True)
     pl.when(follows)(lambda: prev_rest(0))
@@ -434,11 +436,13 @@
     total = nn(fm[0].reshape(NX * MEM, HC), up[0:HC]) + nn(fm[1].reshape(NX * MEM, HC), up[HC:])
     hid[...] = jax.nn.gelu(total, approximate=True).astype(BF).reshape(2, 2 * MEM, FS)
     down = ff[:, :, 1].reshape(D, FS)
-    pc[...] = nt(hid[oc], down).astype(BF)
-    send(pc, pc_in, rs_s.at[0], rs_r.at[0], g, oc)
+    for k in range(2):
+        pc[k] = nt(hid[oc], down[k * HC : (k + 1) * HC]).astype(BF)
+        send(pc.at[k], pc_in.at[k], pc_s.at[k], pc_r.at[k], g, oc)
     own[...] = nt(hid[c], down)
-    arrived(pc_in, rs_r.at[0], rs_s.at[0])
-    own[...] += pc_in[...].astype(F32)
+    for k in range(2):
+        arrived(pc_in.at[k], pc_r.at[k], pc_s.at[k])
+    own[...] += jnp.concatenate([pc_in[0], pc_in[1]], 1).astype(F32)
     for j in range(NX):
         for q in range(2):
             first = q * MEM + j * PART
@@ -513,17 +517,23 @@
     def out_part(cc, h):
         return nn(mx[cc, h], wo[pl.ds(pl.multiple_of(cc * HC + h * HS, HS), HS), :])
 
-    for h in range(HEADS):
+    def cross_head(h):
         cols = slice(h * HS, (h + 1) * HS)
         q = qs[:, :, cols].reshape(2 * HALF, HS)
         scores = nt(q, mk[:, cols])
         high = jnp.max(scores, axis=1, keepdims=True)
         e = jnp.exp2((scores - high) * (SCALE * LOG2E))
         probs = (e / jnp.sum(e, axis=1, keepdims=True)).astype(BF)
-        cross = nn(probs, mv[:, cols])
-        both = lo[:, :, cols].reshape(2 * HALF, HS) + cross
-        mx[c, h] = both.astype(BF)
-        send(mx.at[c, h], mx.at[c, h], mx_s.at[h], mx_r.at[h], g, oc)
+        both = lo[:, :, cols].reshape(2 * HALF, HS) + nn(probs, mv[:, cols])
+        return both.astype(BF)
+
+    for h in range(0, HEADS, 2):
+        pair = [cross_head(h), cross_head(h + 1)]
+        for k in range(2):
+            mx[c, h + k] = pair[k]
+        for k in range(2):
+            b = mx.at[c, h + k]
+            send(b, b, mx_s.at[h + k], mx_r.at[h + k], g, oc)
     acc = out_part(c, 0)
     for h in range(1, HEADS):
         acc += out_part(c, h)
@@ -558,18 +568,18 @@
         V((NZ, ROWS, HS), BF), V((NZ, 8, 128), F32),
         V((2, NX, NX * PART, HC), BF),
         V((NX, 2 * PART, D), BF), V((NX - 1, 2 * PART, D), BF), V((2 * MEM, D), F32),
-        V((2 * MEM, D), BF), V((2 * MEM, D), BF), V((2, 2 * MEM, FS), BF),
+        V((2, 2 * MEM, HC), BF), V((2, 2 * MEM, HC), BF), V((2, 2 * MEM, FS), BF),
         V((2, 2 * PART, D), BF),
         V((2, HALF, HC), F32),
         V((MEM, HC), BF), V((MEM, HC), BF),
         V((2, HEADS, 2 * HALF, HS), BF),
         V((128, 128), F32), V((TAILS, HALF // TAILS, D), BF),
         DMA((8,)), DMA((2,)), DMA((3,)), DMA((3,)), DMA((TAILS,)), DMA((TAILS,)), DMA((TAILS,)), DMA((TAILS,)),
-        DMA((2, NX - 1)), DMA((2, NX - 1)), DMA((2, NZ // 2)), DMA((2, NZ // 2)),
-        DMA((2, NZ)), DMA((2, NZ)), DMA((NZ,)), DMA((NZ,)),
+        DMA((2, NX - 1)), DMA((2, NX - 1)), DMA((2, 2, NZ // 2)), DMA((2, 2, NZ // 2)),
+        DMA((2, NZ)), DMA((2, NZ)), DMA, DMA,
         DMA((2, NX - 1)), DMA((2, NX - 1)), DMA((2, NY - 1)), DMA((2, NY - 1)),
         DMA((2, NZ - 1)), DMA((2, NZ - 1)),
-        DMA((2, NX)), DMA((2, NX)), DMA((NX,)), DMA((NX,)), DMA, DMA, DMA((HEADS,)), DMA((HEADS,)),
+        DMA((2, NX)), DMA((2, NX)), DMA((2,)), DMA((2,)), DMA((NX,)), DMA((NX,)), DMA, DMA, DMA((HEADS,)), DMA((HEADS,)),
     ]
     args = (
         tokens, w_query, w_key, w_value, w_out, slot_query, span_decay, ffn_up,

time: 57 us -> 56.1 us (0.984)
  the two profiles are of different devices: /device:TPU:105 before, /device:TPU:1 now
where the time goes in v4:
time: 56.1 us; the launch traced here: 56 us
  Pallas kernels  55.2 us (98%)
  local copies, waits for them, and re-layouts  0.8 us (1%)
    pallas_call x1, Pallas kernels, shards(): pl.pallas_call(body, out_shape=jax.ShapeDtypeStruct((2 * HALF, HC), BF),...  55.2 us

profile of v4, /device:TPU:1, one launch (start us, length us, event | category | flops | bytes accessed | tf_op | source)
XLA Modules:
  0.0 56.0 jit_solution(17215132184709569566)
XLA Ops:
  0.0 55.2 %shard_map.100 = bf16[512,512]{1,0:T(8,128)(2,1)S(1)} custom-call(bf16[256,1024]{1,0:T(8,128)(2,1)} %tok_h.1, bf16[1024,512]{1,0:T(8,128)(2,1)} %wq_h.1, bf16[1024,512]{1,0:T(8,128)(2,1)} %wk_h.1, bf16[1024,512]{1,0:T(8,128)(2,1)} %wv_h.1, bf16[1024,512]{1,0:T(8,128)(2,1)} %wo_h.1, bf16[64,512]{1,0:T(8,128)(2,1)} %slot_h.1, f32[1,4]{1,0:T(1,128)} %decay_h.1, ...), custom_call_target="tpu_custom_call" | custom-call | tf_op jit(solution)/shard_map/pallas_call | solution.py:590
  55.2 0.8 %copy.12 = bf16[512,512]{1,0:T(8,128)(2,1)} copy(bf16[512,512]{1,0:T(8,128)(2,1)S(1)} %shard_map.100) | data formatting | bytes 1048576

commit v5 on v4

--- a/solution.py
+++ b/solution.py
@@ -153,7 +153,9 @@
 
     pl.semaphore_wait(barrier, 2 * (NX - 1) + (NY - 1) + (NZ - 1) + 5)
 
-    send(tok_h, tok.at[c], tok_s.at[0], tok_r.at[0], g, oc)
+    pieces = ((slice(0, HALF // 2), 0), (slice(HALF // 2, HALF), 3))
+    for r, k in pieces:
+        send(tok_h.at[r], tok.at[c, r], tok_s.at[k], tok_r.at[k], g, oc)
     for k, (src, dst) in enumerate(((up_h, ff), (dn_h, ff))):
         for d in range(1, NX):
             to = xp(d)
@@ -248,8 +250,11 @@
             near_wait(o)
         ring_wait(NZ // 2, far_y, 1)
 
-    arrived(tok.at[oc], tok_r.at[0], tok_s.at[0])
-    project(oc)
+    for r, k in pieces:
+        arrived(tok.at[oc, r], tok_r.at[k], tok_s.at[k])
+        rows = tok[oc, r]
+        ks[oc, r] = nn(rows, wk[...]).astype(BF)
+        vs[oc, r] = nn(rows, wv[...]).astype(BF)
 
     loads[5].wait()
     loads[6].wait()
@@ -574,7 +579,7 @@
         V((MEM, HC), BF), V((MEM, HC), BF),
         V((2, HEADS, 2 * HALF, HS), BF),
         V((128, 128), F32), V((TAILS, HALF // TAILS, D), BF),
-        DMA((8,)), DMA((2,)), DMA((3,)), DMA((3,)), DMA((TAILS,)), DMA((TAILS,)), DMA((TAILS,)), DMA((TAILS,)),
+        DMA((8,)), DMA((2,)), DMA((4,)), DMA((4,)), DMA((TAILS,)), DMA((TAILS,)), DMA((TAILS,)), DMA((TAILS,)),
         DMA((2, NX - 1)), DMA((2, NX - 1)), DMA((2, 2, NZ // 2)), DMA((2, 2, NZ // 2)),
         DMA((2, NZ)), DMA((2, NZ)), DMA, DMA,
         DMA((2, NX - 1)), DMA((2, NX - 1)), DMA((2, NY - 1)), DMA((2, NY - 1)),

time: 56.1 us -> 56 us (level)
  no operation moved by 1% of the time
where the time goes in v5:
time: 56 us
  Pallas kernels  55.2 us (99%)
  local copies, waits for them, and re-layouts  0.8 us (1%)
    pallas_call x1, Pallas kernels, shards(): pl.pallas_call(body, out_shape=jax.ShapeDtypeStruct((2 * HALF, HC), BF),...  55.2 us

profile of v5, /device:TPU:1, one launch (start us, length us, event | category | flops | bytes accessed | tf_op | source)
XLA Modules:
  0.0 56.0 jit_solution(9836807127453998339)
XLA Ops:
  0.0 55.2 %shard_map.100 = bf16[512,512]{1,0:T(8,128)(2,1)S(1)} custom-call(bf16[256,1024]{1,0:T(8,128)(2,1)} %tok_h.1, bf16[1024,512]{1,0:T(8,128)(2,1)} %wq_h.1, bf16[1024,512]{1,0:T(8,128)(2,1)} %wk_h.1, bf16[1024,512]{1,0:T(8,128)(2,1)} %wv_h.1, bf16[1024,512]{1,0:T(8,128)(2,1)} %wo_h.1, bf16[64,512]{1,0:T(8,128)(2,1)} %slot_h.1, f32[1,4]{1,0:T(1,128)} %decay_h.1, ...), custom_call_target="tpu_custom_call" | custom-call | tf_op jit(solution)/shard_map/pallas_call | solution.py:595
  55.2 0.8 %copy.12 = bf16[512,512]{1,0:T(8,128)(2,1)} copy(bf16[512,512]{1,0:T(8,128)(2,1)S(1)} %shard_map.100) | data formatting | bytes 1048576
